TPU v7x, 512 devices: a whole 4x8x8 slice. The times are simulated.
512 devices in a mesh: ingest: 32 (over x, y), section: 16 (over z, core).
Axes of the slice: x: 4, y: 8, z: 8, core: 2. Of those that a mesh axis runs over, the one named last changes fastest.
Arguments:
- txn_feats: bfloat16 [131072, 2048], P(('ingest', 'section')), may hold values from -6 to 6
- txn_seg: int32 [512, 256], P(('ingest', 'section')), may hold values from 0 to 255, as said below
- seg_row: int32 [512, 256], P(('ingest', 'section')), may hold values from 0 to 15, as said below
- send_counts: int32 [512, 32], P(('ingest', 'section')), may hold values from 0 to 8, as said below
- gains: float32 [16, 2048], P('section'), may hold values from 0.5 to 1.5
- tower_w: bfloat16 [16, 2048, 2048], P('section', 'ingest'), may hold values from -0.125 to 0.125
Outputs:
- card_embed: bfloat16 [8192, 2048], P(('ingest', 'section'))
Inputs may be any that keep to these rules, and one draw needn't show every extreme that they name: Each row of send_counts is at most 8 everywhere; in each section index one owner index gets exactly 8 from every device of that section; device 0 sends exactly 8 to every owner. Within a device's row txn_seg never falls, starts at 0 and ends at that device's sum of send_counts minus one. `seg_row`: the segments that one device sends to one owner name different card rows.
All inputs are finite; a program needn't handle non-finite values.
Results may differ from a plain program's by a relative error of at most 0.012.
Values may be sent and summed in bfloat16 or wider, within the bound.
No kernel may reach another device: no remote copies, remote signals or barrier semaphores. Data moves between devices by JAX's collectives and lax.ppermute only.
A program may use at most 64 MiB of HBM per device.

v0:
```python
import jax
import jax.numpy as jnp
from jax import lax
from jax.sharding import PartitionSpec as P

CARD_DEV = 16


def in_one_piece(arrays, axis, split_dim, concat_dim, along):
    columns = [a.reshape(*a.shape[:along], -1) for a in arrays]
    both = jnp.concatenate(columns, axis=along)
    out, at, finished = (
        lax.all_to_all(both, axis, split_axis=split_dim, concat_axis=concat_dim, tiled=True),
        0,
        [],
    )
    for a, column in zip(arrays, columns):
        slab = out[..., at : at + column.shape[along]]
        finished.append(slab.reshape(*slab.shape[:along], *a.shape[along:]))
        at += column.shape[along]
    return tuple(finished)


def laid_out(parts, dim):
    parts = jnp.moveaxis(parts, 0, dim)
    lengths = parts.shape
    return parts.reshape(*lengths[:dim], lengths[dim] * lengths[dim + 1], *lengths[dim + 2 :])


def from_everyone(x, axis):
    count = lax.axis_size(axis)
    return lax.all_to_all(jnp.broadcast_to(x[None], (count, *x.shape)), axis, 0, 0, tiled=True)


def collect(x, axis, dim):
    return laid_out(from_everyone(x, axis), dim)


def from_behind(x, axis, by):
    count = lax.axis_size(axis)
    pairs = [(i, i + by) for i in range(count) if 0 <= i + by < count]
    return lax.ppermute(x, axis, pairs)


def padded_to(lines, count):
    spare = -len(lines) % count
    return jnp.pad(lines, [(0, spare)] + [(0, 0)] * (lines.ndim - 1))


def broadcast_by_parts(x, axis, root):
    lines = jnp.where(lax.axis_index(axis) == root, x, jnp.zeros_like(x)).reshape(
        -1, *x.shape[1:][-1:]
    )
    padded = padded_to(lines, lax.axis_size(axis))
    own = lax.psum_scatter(padded, axis, scatter_dimension=0, tiled=True)
    return lax.all_gather(own, axis, axis=0, tiled=True)[: len(lines)].reshape(x.shape)


def tower_layer(x, gain, weight):
    u = x.astype(jnp.float32)
    mean_sq = jnp.mean(u * u, axis=-1, keepdims=True)
    normed = (u * lax.rsqrt(mean_sq + 1e-05) * gain).astype(jnp.bfloat16)
    y = jnp.dot(normed, weight, preferred_element_type=jnp.float32)
    return (u + jax.nn.silu(y)).astype(jnp.bfloat16)


def body(txn_feats, txn_seg, seg_row, send_counts, gains, tower_w):
    width = txn_feats.shape[1]
    owners = lax.axis_size("ingest")
    sections = lax.axis_size("section")
    slots = seg_row.shape[1]
    cap = slots // owners
    cards = CARD_DEV
    weight = lax.all_gather(tower_w[0], "ingest", axis=0, tiled=True)
    gain = gains[0]
    counts = send_counts[0]
    ends = jnp.cumsum(counts)
    starts = ends - counts
    seg = txn_seg[0]
    rows = seg_row[0]
    owner_ids = jnp.arange(owners, dtype=jnp.int32)
    slot_ids = jnp.arange(slots, dtype=jnp.int32)
    txn_owner = jnp.sum((seg[:, None] >= ends[None, :]).astype(jnp.int32), axis=1)
    owner_hot = (txn_owner[:, None] == owner_ids[None, :]).astype(jnp.int32)
    txn_start = jnp.sum(owner_hot * starts[None, :], axis=1)
    target = txn_owner * cap + seg - txn_start
    place = (slot_ids[:, None] == target[None, :]).astype(jnp.bfloat16)
    buffer = jnp.dot(place, txn_feats, preferred_element_type=jnp.float32).astype(jnp.bfloat16)
    buffer = buffer.reshape(owners, cap, width)
    slot_owner = slot_ids // cap
    slot_rank = slot_ids % cap
    slot_hot = (slot_owner[:, None] == owner_ids[None, :]).astype(jnp.int32)
    seg_of_slot = jnp.sum(slot_hot * starts[None, :], axis=1) + slot_rank
    live = slot_rank < jnp.sum(slot_hot * counts[None, :], axis=1)
    row_of_slot = jnp.sum(
        (seg_of_slot[:, None] == slot_ids[None, :]).astype(jnp.int32) * rows[None, :], axis=1
    )
    labels = jnp.where(live, row_of_slot, -1).astype(jnp.bfloat16).reshape(owners, cap)
    got_rows, got_labels = in_one_piece((buffer, labels), "ingest", 0, 0, 2)
    card_ids = jnp.arange(cards, dtype=jnp.float32)
    pick = (got_labels.reshape(-1).astype(jnp.float32)[None, :] == card_ids[:, None]).astype(
        jnp.bfloat16
    )
    pooled = jnp.dot(pick, got_rows.reshape(-1, width), preferred_element_type=jnp.float32).astype(
        jnp.bfloat16
    )
    section_pos = lax.axis_index("section")
    total_steps = 2 * sections - 1
    blocks = collect(pooled[None], "section", 0)

    def advance(step, carry):
        current, finished, waiting = carry
        incoming = from_behind(current, "section", 1)
        fresh = lax.dynamic_index_in_dim(blocks, jnp.minimum(step, sections - 1), 0, keepdims=False)
        entry = jnp.where(section_pos == 0, fresh, incoming)
        active = (step >= section_pos) & (step < section_pos + sections)
        result = lax.cond(active, lambda v: tower_layer(v, gain, weight), lambda v: v, entry)
        place_at = jnp.clip(step - (sections - 1), 0, sections - 1)
        keep = (section_pos == sections - 1) & (step >= sections - 1)
        before = lax.dynamic_index_in_dim(finished, place_at, 0, keepdims=False)
        finished = lax.dynamic_update_index_in_dim(
            finished, jnp.where(keep, result, before), place_at, 0
        )
        return (result, finished, waiting)

    start_state = (
        jnp.zeros_like(pooled),
        jnp.zeros((sections, cards, width), jnp.bfloat16),
        pooled,
    )
    final_state = lax.fori_loop(0, total_steps, advance, start_state)
    everything = broadcast_by_parts(final_state[1], "section", sections - 1)
    return lax.dynamic_index_in_dim(everything, section_pos, 0, keepdims=False)


def solution(mesh):
    in_specs = (
        P(("ingest", "section"), None),
        P(("ingest", "section"), None),
        P(("ingest", "section"), None),
        P(("ingest", "section"), None),
        P("section", None),
        P("section", "ingest", None),
    )
    out_specs = P(("ingest", "section"), None)
    return jax.shard_map(body, mesh=mesh, in_specs=in_specs, out_specs=out_specs, check_vma=False)
```

profile of v0, /device:TPU:1, one launch (start us, length us, event | category | flops | bytes accessed | tf_op | source)
XLA Modules:
  0.0 546.4 jit_solution(16966570204640566806)
XLA Ops:
  13.0 46.7 %all_to_all.10 = bf16[32,8,2049]{2,1,0:T(8,128)(2,1)S(1)} all-to-all(bf16[32,8,2049]{2,1,0:T(8,128)(2,1)S(1)} %pad_maximum_fusion), channel_id=1, replica_groups=mesh['ingest'=32,'section'=16] {'ingest'}, dimensions={0} | all-to-all | bytes 2098176 | tf_op jit(solution)/shard_map/all_to_all | solution.py:13
  61.4 15.4 %all-to-all-start.1 = ((bf16[16,1,16,2048]{3,2,1,0:T(8,128)(2,1)}), bf16[16,1,16,2048]{3,2,1,0:T(8,128)(2,1)S(1)}, u32[]{:S(2)}, u32[]{:S(2)}) async-start(bf16[16,1,16,2048]{3,2,1,0:T(8,128)(2,1)} %broadcast_in_dim.21), calls=%async_computation.1 | async-start | bytes 2097152 | tf_op jit(solution)/shard_map/all_to_all | solution.py:32
  76.9 27.9 %all-to-all-done.1 = bf16[16,1,16,2048]{3,2,1,0:T(8,128)(2,1)S(1)} async-done(((bf16[16,1,16,2048]{3,2,1,0:T(8,128)(2,1)}), bf16[16,1,16,2048]{3,2,1,0:T(8,128)(2,1)S(1)}, u32[]{:S(2)}, u32[]{:S(2)}) %all-to-all-start.1) | async-done | bytes 1048608 | tf_op jit(solution)/shard_map/all_to_all | solution.py:32
  104.8 21.8 %all-gather.6.cloned.1.call-done = bf16[1,2048,2048]{2,1,0:T(8,128)(2,1)} async-done(((bf16[1,64,2048]{2,1,0:T(8,128)(2,1)}), bf16[1,2048,2048]{2,1,0:T(8,128)(2,1)}) %all-gather.6.cloned.1.call-update) | async-done | bytes 8388624 | tf_op jit(solution)/shard_map/all_gather | solution.py:74
  126.7 280.7 %while.17 = (s32[]{:T(128)}, bf16[16,2048]{1,0:T(8,128)(2,1)S(1)}, bf16[16,16,2048]{2,1,0:T(8,128)(2,1)S(1)}, s32[]{:T(128)}, s32[]{:T(128)}, /*index=5*/pred[]{...) while((s32[]{:T(128)}, bf16[16,2048]{1,0:T(8,128)(2,1)S(1)}, ...), condition=%wide.region_10.11_spmd, body=%wide.region_6.10_spmd.sunk | while | flops 134742048 | bytes 9511515 | solution.py:131
  138.3 4.8 conditional.2
  146.4 4.8 conditional.2
  156.9 4.8 conditional.2
  167.4 4.8 conditional.2
  177.8 4.8 conditional.2
  188.3 4.8 conditional.2
  198.8 4.8 conditional.2
  282.5 4.8 conditional.2
  303.5 9.1 %collective-permute-start = (bf16[16,2048]{1,0:T(8,128)(2,1)S(1)}, bf16[16,2048]{1,0:T(8,128)(2,1)S(1)}, u32[]{:S(2)}, u32[]{:S(2)}) collective-permute-start(bf16[16,2048]{1,0:T(8,128)(2,1)S(1)} %get-tuple-element.318), channel_id=1, source_target_pairs={{0,1},{1,2},{2,3},{3,4},{4,5},{5,6},{6,7},{7,8},{8,9},{9,10},{10,1... | collective-permute-start | bytes 196616 | tf_op jit(solution)/shard_map/while/body/eval_jaxpr/ppermute | solution.py:42
  331.0 6.3 %collective-permute-start = (bf16[16,2048]{1,0:T(8,128)(2,1)S(1)}, bf16[16,2048]{1,0:T(8,128)(2,1)S(1)}, u32[]{:S(2)}, u32[]{:S(2)}) collective-permute-start(bf16[16,2048]{1,0:T(8,128)(2,1)S(1)} %get-tuple-element.318), channel_id=1, source_target_pairs={{0,1},{1,2},{2,3},{3,4},{4,5},{5,6},{6,7},{7,8},{8,9},{9,10},{10,1... | collective-permute-start | bytes 196616 | tf_op jit(solution)/shard_map/while/body/eval_jaxpr/ppermute | solution.py:42
  344.4 6.1 %collective-permute-start = (bf16[16,2048]{1,0:T(8,128)(2,1)S(1)}, bf16[16,2048]{1,0:T(8,128)(2,1)S(1)}, u32[]{:S(2)}, u32[]{:S(2)}) collective-permute-start(bf16[16,2048]{1,0:T(8,128)(2,1)S(1)} %get-tuple-element.318), channel_id=1, source_target_pairs={{0,1},{1,2},{2,3},{3,4},{4,5},{5,6},{6,7},{7,8},{8,9},{9,10},{10,1... | collective-permute-start | bytes 196616 | tf_op jit(solution)/shard_map/while/body/eval_jaxpr/ppermute | solution.py:42
  351.8 5.5 %collective-permute-start = (bf16[16,2048]{1,0:T(8,128)(2,1)S(1)}, bf16[16,2048]{1,0:T(8,128)(2,1)S(1)}, u32[]{:S(2)}, u32[]{:S(2)}) collective-permute-start(bf16[16,2048]{1,0:T(8,128)(2,1)S(1)} %get-tuple-element.318), channel_id=1, source_target_pairs={{0,1},{1,2},{2,3},{3,4},{4,5},{5,6},{6,7},{7,8},{8,9},{9,10},{10,1... | collective-permute-start | bytes 196616 | tf_op jit(solution)/shard_map/while/body/eval_jaxpr/ppermute | solution.py:42
  358.7 10.3 %collective-permute-start = (bf16[16,2048]{1,0:T(8,128)(2,1)S(1)}, bf16[16,2048]{1,0:T(8,128)(2,1)S(1)}, u32[]{:S(2)}, u32[]{:S(2)}) collective-permute-start(bf16[16,2048]{1,0:T(8,128)(2,1)S(1)} %get-tuple-element.318), channel_id=1, source_target_pairs={{0,1},{1,2},{2,3},{3,4},{4,5},{5,6},{6,7},{7,8},{8,9},{9,10},{10,1... | collective-permute-start | bytes 196616 | tf_op jit(solution)/shard_map/while/body/eval_jaxpr/ppermute | solution.py:42
  370.4 5.5 %collective-permute-start = (bf16[16,2048]{1,0:T(8,128)(2,1)S(1)}, bf16[16,2048]{1,0:T(8,128)(2,1)S(1)}, u32[]{:S(2)}, u32[]{:S(2)}) collective-permute-start(bf16[16,2048]{1,0:T(8,128)(2,1)S(1)} %get-tuple-element.318), channel_id=1, source_target_pairs={{0,1},{1,2},{2,3},{3,4},{4,5},{5,6},{6,7},{7,8},{8,9},{9,10},{10,1... | collective-permute-start | bytes 196616 | tf_op jit(solution)/shard_map/while/body/eval_jaxpr/ppermute | solution.py:42
  377.2 10.3 %collective-permute-start = (bf16[16,2048]{1,0:T(8,128)(2,1)S(1)}, bf16[16,2048]{1,0:T(8,128)(2,1)S(1)}, u32[]{:S(2)}, u32[]{:S(2)}) collective-permute-start(bf16[16,2048]{1,0:T(8,128)(2,1)S(1)} %get-tuple-element.318), channel_id=1, source_target_pairs={{0,1},{1,2},{2,3},{3,4},{4,5},{5,6},{6,7},{7,8},{8,9},{9,10},{10,1... | collective-permute-start | bytes 196616 | tf_op jit(solution)/shard_map/while/body/eval_jaxpr/ppermute | solution.py:42
  388.9 5.5 %collective-permute-start = (bf16[16,2048]{1,0:T(8,128)(2,1)S(1)}, bf16[16,2048]{1,0:T(8,128)(2,1)S(1)}, u32[]{:S(2)}, u32[]{:S(2)}) collective-permute-start(bf16[16,2048]{1,0:T(8,128)(2,1)S(1)} %get-tuple-element.318), channel_id=1, source_target_pairs={{0,1},{1,2},{2,3},{3,4},{4,5},{5,6},{6,7},{7,8},{8,9},{9,10},{10,1... | collective-permute-start | bytes 196616 | tf_op jit(solution)/shard_map/while/body/eval_jaxpr/ppermute | solution.py:42
  395.8 10.3 %collective-permute-start = (bf16[16,2048]{1,0:T(8,128)(2,1)S(1)}, bf16[16,2048]{1,0:T(8,128)(2,1)S(1)}, u32[]{:S(2)}, u32[]{:S(2)}) collective-permute-start(bf16[16,2048]{1,0:T(8,128)(2,1)S(1)} %get-tuple-element.318), channel_id=1, source_target_pairs={{0,1},{1,2},{2,3},{3,4},{4,5},{5,6},{6,7},{7,8},{8,9},{9,10},{10,1... | collective-permute-start | bytes 196616 | tf_op jit(solution)/shard_map/while/body/eval_jaxpr/ppermute | solution.py:42
  408.6 84.8 %reduce-scatter.2.cloned.1.call-done = bf16[16,2048]{1,0:T(8,128)(2,1)} async-done(((bf16[256,2048]{1,0:T(8,128)(2,1)}), bf16[16,2048]{1,0:T(8,128)(2,1)}) %reduce-scatter.2.cloned.1.call-update) | async-done | bytes 65552 | tf_op jit(solution)/shard_map/reduce_scatter | solution.py:55
  493.4 45.0 %all-gather.4.cloned.1.call-done = bf16[256,2048]{1,0:T(8,128)(2,1)} async-done(((bf16[16,2048]{1,0:T(8,128)(2,1)}), bf16[256,2048]{1,0:T(8,128)(2,1)}) %all-gather.4.cloned.1.call-update) | async-done | bytes 1048592 | tf_op jit(solution)/shard_map/all_gather | solution.py:56
  (270 shorter events, 258.3 us)
Async XLA Ops:
  6.5 120.1 %all-gather.6.cloned.1.call-start = ((), (), s32[]{:S(2)}) async-start(), calls=%async_computation.5 | async-start | bytes 8650752 | tf_op jit(solution)/shard_map/all_gather | solution.py:74
  61.4 43.4 %all-to-all-start.1 = ((bf16[16,1,16,2048]{3,2,1,0:T(8,128)(2,1)}), bf16[16,1,16,2048]{3,2,1,0:T(8,128)(2,1)S(1)}, u32[]{:S(2)}, u32[]{:S(2)}) async-start(bf16[16,1,16,2048]{3,2,1,0:T(8,128)(2,1)} %broadcast_in_dim.21), calls=%async_computation.1 | async-start | bytes 2097152 | tf_op jit(solution)/shard_map/all_to_all | solution.py:32
  76.8 416.6 %reduce-scatter.2.cloned.1.call-start = ((), (), s32[]{:S(2)}) async-start(), calls=%async_computation.3 | async-start | bytes 1114112 | tf_op jit(solution)/shard_map/reduce_scatter | solution.py:55
  126.8 5.9 %collective-permute-start = (bf16[16,2048]{1,0:T(8,128)(2,1)S(1)}, bf16[16,2048]{1,0:T(8,128)(2,1)S(1)}, u32[]{:S(2)}, u32[]{:S(2)}) collective-permute-start(bf16[16,2048]{1,0:T(8,128)(2,1)S(1)} %get-tuple-element.318), channel_id=1, source_target_pairs={{0,1},{1,2},{2,3},{3,4},{4,5},{5,6},{6,7},{7,8},{8,9},{9,10},{10,1... | collective-permute-start | bytes 196616 | tf_op jit(solution)/shard_map/while/body/eval_jaxpr/ppermute | solution.py:42
  132.7 5.6 %collective-permute-start = (bf16[16,2048]{1,0:T(8,128)(2,1)S(1)}, bf16[16,2048]{1,0:T(8,128)(2,1)S(1)}, u32[]{:S(2)}, u32[]{:S(2)}) collective-permute-start(bf16[16,2048]{1,0:T(8,128)(2,1)S(1)} %get-tuple-element.318), channel_id=1, source_target_pairs={{0,1},{1,2},{2,3},{3,4},{4,5},{5,6},{6,7},{7,8},{8,9},{9,10},{10,1... | collective-permute-start | bytes 196616 | tf_op jit(solution)/shard_map/while/body/eval_jaxpr/ppermute | solution.py:42
  151.3 5.6 %collective-permute-start = (bf16[16,2048]{1,0:T(8,128)(2,1)S(1)}, bf16[16,2048]{1,0:T(8,128)(2,1)S(1)}, u32[]{:S(2)}, u32[]{:S(2)}) collective-permute-start(bf16[16,2048]{1,0:T(8,128)(2,1)S(1)} %get-tuple-element.318), channel_id=1, source_target_pairs={{0,1},{1,2},{2,3},{3,4},{4,5},{5,6},{6,7},{7,8},{8,9},{9,10},{10,1... | collective-permute-start | bytes 196616 | tf_op jit(solution)/shard_map/while/body/eval_jaxpr/ppermute | solution.py:42
  161.8 5.6 %collective-permute-start = (bf16[16,2048]{1,0:T(8,128)(2,1)S(1)}, bf16[16,2048]{1,0:T(8,128)(2,1)S(1)}, u32[]{:S(2)}, u32[]{:S(2)}) collective-permute-start(bf16[16,2048]{1,0:T(8,128)(2,1)S(1)} %get-tuple-element.318), channel_id=1, source_target_pairs={{0,1},{1,2},{2,3},{3,4},{4,5},{5,6},{6,7},{7,8},{8,9},{9,10},{10,1... | collective-permute-start | bytes 196616 | tf_op jit(solution)/shard_map/while/body/eval_jaxpr/ppermute | solution.py:42
  172.2 5.6 %collective-permute-start = (bf16[16,2048]{1,0:T(8,128)(2,1)S(1)}, bf16[16,2048]{1,0:T(8,128)(2,1)S(1)}, u32[]{:S(2)}, u32[]{:S(2)}) collective-permute-start(bf16[16,2048]{1,0:T(8,128)(2,1)S(1)} %get-tuple-element.318), channel_id=1, source_target_pairs={{0,1},{1,2},{2,3},{3,4},{4,5},{5,6},{6,7},{7,8},{8,9},{9,10},{10,1... | collective-permute-start | bytes 196616 | tf_op jit(solution)/shard_map/while/body/eval_jaxpr/ppermute | solution.py:42
  182.7 5.6 %collective-permute-start = (bf16[16,2048]{1,0:T(8,128)(2,1)S(1)}, bf16[16,2048]{1,0:T(8,128)(2,1)S(1)}, u32[]{:S(2)}, u32[]{:S(2)}) collective-permute-start(bf16[16,2048]{1,0:T(8,128)(2,1)S(1)} %get-tuple-element.318), channel_id=1, source_target_pairs={{0,1},{1,2},{2,3},{3,4},{4,5},{5,6},{6,7},{7,8},{8,9},{9,10},{10,1... | collective-permute-start | bytes 196616 | tf_op jit(solution)/shard_map/while/body/eval_jaxpr/ppermute | solution.py:42
  193.2 5.6 %collective-permute-start = (bf16[16,2048]{1,0:T(8,128)(2,1)S(1)}, bf16[16,2048]{1,0:T(8,128)(2,1)S(1)}, u32[]{:S(2)}, u32[]{:S(2)}) collective-permute-start(bf16[16,2048]{1,0:T(8,128)(2,1)S(1)} %get-tuple-element.318), channel_id=1, source_target_pairs={{0,1},{1,2},{2,3},{3,4},{4,5},{5,6},{6,7},{7,8},{8,9},{9,10},{10,1... | collective-permute-start | bytes 196616 | tf_op jit(solution)/shard_map/while/body/eval_jaxpr/ppermute | solution.py:42
  276.9 5.6 %collective-permute-start = (bf16[16,2048]{1,0:T(8,128)(2,1)S(1)}, bf16[16,2048]{1,0:T(8,128)(2,1)S(1)}, u32[]{:S(2)}, u32[]{:S(2)}) collective-permute-start(bf16[16,2048]{1,0:T(8,128)(2,1)S(1)} %get-tuple-element.318), channel_id=1, source_target_pairs={{0,1},{1,2},{2,3},{3,4},{4,5},{5,6},{6,7},{7,8},{8,9},{9,10},{10,1... | collective-permute-start | bytes 196616 | tf_op jit(solution)/shard_map/while/body/eval_jaxpr/ppermute | solution.py:42
  303.5 10.4 %collective-permute-start = (bf16[16,2048]{1,0:T(8,128)(2,1)S(1)}, bf16[16,2048]{1,0:T(8,128)(2,1)S(1)}, u32[]{:S(2)}, u32[]{:S(2)}) collective-permute-start(bf16[16,2048]{1,0:T(8,128)(2,1)S(1)} %get-tuple-element.318), channel_id=1, source_target_pairs={{0,1},{1,2},{2,3},{3,4},{4,5},{5,6},{6,7},{7,8},{8,9},{9,10},{10,1... | collective-permute-start | bytes 196616 | tf_op jit(solution)/shard_map/while/body/eval_jaxpr/ppermute | solution.py:42
  314.0 5.6 %collective-permute-start = (bf16[16,2048]{1,0:T(8,128)(2,1)S(1)}, bf16[16,2048]{1,0:T(8,128)(2,1)S(1)}, u32[]{:S(2)}, u32[]{:S(2)}) collective-permute-start(bf16[16,2048]{1,0:T(8,128)(2,1)S(1)} %get-tuple-element.318), channel_id=1, source_target_pairs={{0,1},{1,2},{2,3},{3,4},{4,5},{5,6},{6,7},{7,8},{8,9},{9,10},{10,1... | collective-permute-start | bytes 196616 | tf_op jit(solution)/shard_map/while/body/eval_jaxpr/ppermute | solution.py:42
  319.7 5.6 %collective-permute-start = (bf16[16,2048]{1,0:T(8,128)(2,1)S(1)}, bf16[16,2048]{1,0:T(8,128)(2,1)S(1)}, u32[]{:S(2)}, u32[]{:S(2)}) collective-permute-start(bf16[16,2048]{1,0:T(8,128)(2,1)S(1)} %get-tuple-element.318), channel_id=1, source_target_pairs={{0,1},{1,2},{2,3},{3,4},{4,5},{5,6},{6,7},{7,8},{8,9},{9,10},{10,1... | collective-permute-start | bytes 196616 | tf_op jit(solution)/shard_map/while/body/eval_jaxpr/ppermute | solution.py:42
  325.3 5.6 %collective-permute-start = (bf16[16,2048]{1,0:T(8,128)(2,1)S(1)}, bf16[16,2048]{1,0:T(8,128)(2,1)S(1)}, u32[]{:S(2)}, u32[]{:S(2)}) collective-permute-start(bf16[16,2048]{1,0:T(8,128)(2,1)S(1)} %get-tuple-element.318), channel_id=1, source_target_pairs={{0,1},{1,2},{2,3},{3,4},{4,5},{5,6},{6,7},{7,8},{8,9},{9,10},{10,1... | collective-permute-start | bytes 196616 | tf_op jit(solution)/shard_map/while/body/eval_jaxpr/ppermute | solution.py:42
  331.0 7.6 %collective-permute-start = (bf16[16,2048]{1,0:T(8,128)(2,1)S(1)}, bf16[16,2048]{1,0:T(8,128)(2,1)S(1)}, u32[]{:S(2)}, u32[]{:S(2)}) collective-permute-start(bf16[16,2048]{1,0:T(8,128)(2,1)S(1)} %get-tuple-element.318), channel_id=1, source_target_pairs={{0,1},{1,2},{2,3},{3,4},{4,5},{5,6},{6,7},{7,8},{8,9},{9,10},{10,1... | collective-permute-start | bytes 196616 | tf_op jit(solution)/shard_map/while/body/eval_jaxpr/ppermute | solution.py:42
  344.4 7.4 %collective-permute-start = (bf16[16,2048]{1,0:T(8,128)(2,1)S(1)}, bf16[16,2048]{1,0:T(8,128)(2,1)S(1)}, u32[]{:S(2)}, u32[]{:S(2)}) collective-permute-start(bf16[16,2048]{1,0:T(8,128)(2,1)S(1)} %get-tuple-element.318), channel_id=1, source_target_pairs={{0,1},{1,2},{2,3},{3,4},{4,5},{5,6},{6,7},{7,8},{8,9},{9,10},{10,1... | collective-permute-start | bytes 196616 | tf_op jit(solution)/shard_map/while/body/eval_jaxpr/ppermute | solution.py:42
  351.8 6.8 %collective-permute-start = (bf16[16,2048]{1,0:T(8,128)(2,1)S(1)}, bf16[16,2048]{1,0:T(8,128)(2,1)S(1)}, u32[]{:S(2)}, u32[]{:S(2)}) collective-permute-start(bf16[16,2048]{1,0:T(8,128)(2,1)S(1)} %get-tuple-element.318), channel_id=1, source_target_pairs={{0,1},{1,2},{2,3},{3,4},{4,5},{5,6},{6,7},{7,8},{8,9},{9,10},{10,1... | collective-permute-start | bytes 196616 | tf_op jit(solution)/shard_map/while/body/eval_jaxpr/ppermute | solution.py:42
  358.7 11.6 %collective-permute-start = (bf16[16,2048]{1,0:T(8,128)(2,1)S(1)}, bf16[16,2048]{1,0:T(8,128)(2,1)S(1)}, u32[]{:S(2)}, u32[]{:S(2)}) collective-permute-start(bf16[16,2048]{1,0:T(8,128)(2,1)S(1)} %get-tuple-element.318), channel_id=1, source_target_pairs={{0,1},{1,2},{2,3},{3,4},{4,5},{5,6},{6,7},{7,8},{8,9},{9,10},{10,1... | collective-permute-start | bytes 196616 | tf_op jit(solution)/shard_map/while/body/eval_jaxpr/ppermute | solution.py:42
  370.4 6.8 %collective-permute-start = (bf16[16,2048]{1,0:T(8,128)(2,1)S(1)}, bf16[16,2048]{1,0:T(8,128)(2,1)S(1)}, u32[]{:S(2)}, u32[]{:S(2)}) collective-permute-start(bf16[16,2048]{1,0:T(8,128)(2,1)S(1)} %get-tuple-element.318), channel_id=1, source_target_pairs={{0,1},{1,2},{2,3},{3,4},{4,5},{5,6},{6,7},{7,8},{8,9},{9,10},{10,1... | collective-permute-start | bytes 196616 | tf_op jit(solution)/shard_map/while/body/eval_jaxpr/ppermute | solution.py:42
  377.2 11.6 %collective-permute-start = (bf16[16,2048]{1,0:T(8,128)(2,1)S(1)}, bf16[16,2048]{1,0:T(8,128)(2,1)S(1)}, u32[]{:S(2)}, u32[]{:S(2)}) collective-permute-start(bf16[16,2048]{1,0:T(8,128)(2,1)S(1)} %get-tuple-element.318), channel_id=1, source_target_pairs={{0,1},{1,2},{2,3},{3,4},{4,5},{5,6},{6,7},{7,8},{8,9},{9,10},{10,1... | collective-permute-start | bytes 196616 | tf_op jit(solution)/shard_map/while/body/eval_jaxpr/ppermute | solution.py:42
  388.9 6.8 %collective-permute-start = (bf16[16,2048]{1,0:T(8,128)(2,1)S(1)}, bf16[16,2048]{1,0:T(8,128)(2,1)S(1)}, u32[]{:S(2)}, u32[]{:S(2)}) collective-permute-start(bf16[16,2048]{1,0:T(8,128)(2,1)S(1)} %get-tuple-element.318), channel_id=1, source_target_pairs={{0,1},{1,2},{2,3},{3,4},{4,5},{5,6},{6,7},{7,8},{8,9},{9,10},{10,1... | collective-permute-start | bytes 196616 | tf_op jit(solution)/shard_map/while/body/eval_jaxpr/ppermute | solution.py:42
  395.8 11.6 %collective-permute-start = (bf16[16,2048]{1,0:T(8,128)(2,1)S(1)}, bf16[16,2048]{1,0:T(8,128)(2,1)S(1)}, u32[]{:S(2)}, u32[]{:S(2)}) collective-permute-start(bf16[16,2048]{1,0:T(8,128)(2,1)S(1)} %get-tuple-element.318), channel_id=1, source_target_pairs={{0,1},{1,2},{2,3},{3,4},{4,5},{5,6},{6,7},{7,8},{8,9},{9,10},{10,1... | collective-permute-start | bytes 196616 | tf_op jit(solution)/shard_map/while/body/eval_jaxpr/ppermute | solution.py:42
  408.6 129.9 %all-gather.4.cloned.1.call-start = ((), (), s32[]{:S(2)}) async-start(), calls=%async_computation.4 | async-start | bytes 1114112 | tf_op jit(solution)/shard_map/all_gather | solution.py:56
  (13 other events, 131.6 us)
Sparse Core Ops, SparseCore 0:
  10.5 116.0 all-gather.5
  408.7 84.6 reduce-scatter.1
  495.5 42.8 all-gather.3
where the time goes:
time: 548 us; the launch traced here: 546 us
  waiting for transfers between devices  219 us (40%)
  starting transfers between devices  176 us (32%)
  matrix products  75 us (14%)
  blocking collectives  46.7 us (9%)
  between operations  13.2 us (2%)
  other arithmetic  8.42 us (2%)
    ppermute x31, starting transfers between devices, from_behind(): return lax.ppermute(x, axis, pairs)  161 us
    reduce_scatter x1, waiting for transfers between devices, broadcast_by_parts(): own = lax.psum_scatter(padded, axis, scatter_dimension=0, tiled=True)  84.8 us
    dot_general x16, matrix products, tower_layer(): y = jnp.dot(normed, weight, preferred_element_type=jnp.float32)  74.3 us
    all_to_all x1, blocking collectives, in_one_piece(): lax.all_to_all(both, axis, split_axis=split_dim, concat_axis=concat_dim,...  46.7 us
    all_gather x1, waiting for transfers between devices, broadcast_by_parts(): lax.all_gather(own, axis, axis=0, tiled=True)[:len(lines)].reshape(x.shape)  45 us
    ppermute x31, waiting for transfers between devices, from_behind(): return lax.ppermute(x, axis, pairs)  39 us
    all_to_all x1, waiting for transfers between devices, from_everyone(): lax.all_to_all(jnp.broadcast_to(x[None], (count, *x.shape)), axis, 0, 0,...  27.9 us
    all_gather x1, waiting for transfers between devices, body(): weight = lax.all_gather(tower_w[0], 'ingest', axis=0, tiled=True)  21.8 us
  transfers between devices with their start and end apart: 35, of which 35 were waited for; matrix products, arithmetic and copies ran while one was open for 1% of the time, Pallas kernels for 0%

commit v1 on v0

v1 whole, which is shorter than its diff:
```python
import functools

import jax
import jax.numpy as jnp
from jax import lax
from jax.experimental import pallas as pl
from jax.experimental.pallas import tpu as pltpu
from jax.sharding import Mesh, PartitionSpec as P

CARD_DEV = 16
X, Y, Z, C = 4, 8, 8, 2
DEVICES = ("x", "y", "z", "c")
LANES = 128
BLOCK = 512
VMEM = pltpu.MemorySpace.VMEM
SMEM = pltpu.MemorySpace.SMEM
MIB = 1024 * 1024


def pool_kernel(counts_ref, seg_ref, rows_ref, feats_ref, out_ref, *, cap):
    owners = counts_ref.shape[1]
    slots = rows_ref.shape[1]
    txns, width = feats_ref.shape
    counts = counts_ref[...]
    below = lax.broadcasted_iota(jnp.int32, (owners, owners), 0)
    across = lax.broadcasted_iota(jnp.int32, (owners, owners), 1)
    counts_all = jnp.broadcast_to(counts, (owners, owners))
    starts_col = jnp.sum(jnp.where(across < below, counts_all, 0), axis=1, keepdims=True)
    counts_col = jnp.sum(jnp.where(across == below, counts_all, 0), axis=1, keepdims=True)
    ends_col = starts_col + counts_col
    starts_row = jnp.sum(
        jnp.where(below < across, jnp.broadcast_to(counts_col, (owners, owners)), 0),
        axis=0,
        keepdims=True,
    )
    seg = seg_ref[...]
    ids = lax.broadcasted_iota(jnp.int32, (owners, txns), 0)
    owner = jnp.sum((seg >= ends_col).astype(jnp.int32), axis=0, keepdims=True)
    start = jnp.sum(jnp.where(ids == owner, starts_col, 0), axis=0, keepdims=True)
    target = owner * cap + seg - start
    slot = lax.broadcasted_iota(jnp.int32, (slots, txns), 0)
    place = (slot == target).astype(jnp.float32).astype(jnp.bfloat16)
    part = jnp.dot(place, feats_ref[...], preferred_element_type=jnp.float32)
    out_ref[:, :width] = part.astype(jnp.bfloat16)
    slot_col = lax.broadcasted_iota(jnp.int32, (slots, owners), 0)
    owner_row = lax.broadcasted_iota(jnp.int32, (slots, owners), 1)
    mine = (slot_col // cap) == owner_row
    slot_start = jnp.sum(jnp.where(mine, starts_row, 0), axis=1, keepdims=True)
    slot_count = jnp.sum(jnp.where(mine, counts, 0), axis=1, keepdims=True)
    rank = lax.broadcasted_iota(jnp.int32, (slots, 1), 0) % cap
    named = lax.broadcasted_iota(jnp.int32, (slots, slots), 1) == slot_start + rank
    row = jnp.sum(jnp.where(named, rows_ref[...], 0), axis=1, keepdims=True)
    label = jnp.where(rank < slot_count, row, -1)
    out_ref[:, width:] = jnp.broadcast_to(
        label.astype(jnp.float32), (slots, LANES)
    ).astype(jnp.bfloat16)


def pool(counts, seg, rows, feats):
    slots = rows.shape[1]
    width = feats.shape[1]
    cap = slots // counts.shape[1]
    return pl.pallas_call(
        functools.partial(pool_kernel, cap=cap),
        out_shape=jax.ShapeDtypeStruct((slots, width + LANES), jnp.bfloat16),
        in_specs=[pl.BlockSpec(memory_space=VMEM)] * 4,
        out_specs=pl.BlockSpec(memory_space=VMEM),
        compiler_params=pltpu.CompilerParams(vmem_limit_bytes=24 * MIB),
        name="pool",
    )(counts, seg, rows, feats)


def pick_kernel(got_ref, out_ref, *, cards, cap, groups):
    senders, slots, wide = got_ref.shape
    width = wide - LANES
    total = senders * slots
    got = got_ref[...].reshape(total, wide)
    label = got[:, width : width + 1].astype(jnp.float32).astype(jnp.int32)
    slot = lax.broadcasted_iota(jnp.int32, (total, 1), 0)
    card = jnp.where(label >= 0, ((slot // cap) % groups) * cards + label, -1)
    ids = lax.broadcasted_iota(jnp.int32, (total, groups * cards), 1)
    hot = (ids == card).astype(jnp.float32).astype(jnp.bfloat16)
    out = lax.dot_general(
        hot, got[:, :width], (((0,), (0,)), ((), ())), preferred_element_type=jnp.float32
    )
    out_ref[...] = out.astype(jnp.bfloat16)


def pick(got, cap, groups):
    width = got.shape[2] - LANES
    out = pl.pallas_call(
        functools.partial(pick_kernel, cards=CARD_DEV, cap=cap, groups=groups),
        out_shape=jax.ShapeDtypeStruct((groups * CARD_DEV, width), jnp.bfloat16),
        in_specs=[pl.BlockSpec(memory_space=VMEM)],
        out_specs=pl.BlockSpec(memory_space=VMEM),
        compiler_params=pltpu.CompilerParams(vmem_limit_bytes=24 * MIB),
        name="pick",
    )(got)
    return out.reshape(groups, CARD_DEV, width)


def load_kernel(gathered_ref, out_ref, sem):
    blocks, layers, rows, width = gathered_ref.shape
    copies = [
        pltpu.make_async_copy(
            gathered_ref.at[b, layer], out_ref.at[layer, pl.ds(b * rows, rows)], sem.at[b, layer]
        )
        for b in range(blocks)
        for layer in range(layers)
    ]
    for copy in copies:
        copy.start()
    for copy in copies:
        copy.wait()


def load_weights(gathered):
    blocks, layers, rows, width = gathered.shape
    return pl.pallas_call(
        load_kernel,
        out_shape=pltpu.VMEM((layers, blocks * rows, width), jnp.bfloat16),
        in_specs=[pl.BlockSpec(memory_space=pl.ANY)],
        out_specs=pl.BlockSpec(memory_space=VMEM),
        scratch_shapes=[pltpu.SemaphoreType.DMA((blocks, layers))],
        compiler_params=pltpu.CompilerParams(vmem_limit_bytes=20 * MIB),
        name="load_weights",
    )(gathered)


def stage_kernel(position_ref, x_ref, gain_ref, weight_ref, out_ref, normed_ref, *, step):
    active = (step >= position_ref[0]) & (step < position_ref[0] + Z)
    width = x_ref.shape[1]
    out_ref[...] = x_ref[...]

    @pl.when(active)
    def _():
        def layer_of(layer, carry):
            u = out_ref[...].astype(jnp.float32)
            mean_sq = jnp.mean(u * u, axis=-1, keepdims=True)
            normed = u * lax.rsqrt(mean_sq + 1e-05) * gain_ref[pl.ds(layer, 1), :]
            normed_ref[...] = normed.astype(jnp.bfloat16)

            def columns_of(block, carry):
                columns = pl.ds(pl.multiple_of(block * BLOCK, BLOCK), BLOCK)
                y = jnp.dot(
                    normed_ref[...],
                    weight_ref[layer, :, columns],
                    preferred_element_type=jnp.float32,
                )
                u = out_ref[:, columns].astype(jnp.float32)
                out_ref[:, columns] = (u + y / (1.0 + jnp.exp(-y))).astype(jnp.bfloat16)
                return carry

            return lax.fori_loop(0, width // BLOCK, columns_of, carry)

        lax.fori_loop(0, weight_ref.shape[0], layer_of, 0)


def stage(position, x, gain, weight, step):
    return pl.pallas_call(
        functools.partial(stage_kernel, step=step),
        out_shape=jax.ShapeDtypeStruct(x.shape, x.dtype),
        in_specs=[pl.BlockSpec(memory_space=SMEM)] + [pl.BlockSpec(memory_space=VMEM)] * 3,
        out_specs=pl.BlockSpec(memory_space=VMEM),
        scratch_shapes=[pltpu.VMEM(x.shape, jnp.bfloat16)],
        compiler_params=pltpu.CompilerParams(vmem_limit_bytes=24 * MIB),
        name="stage",
    )(position, x, gain, weight)


def body(txn_feats, txn_seg, seg_row, send_counts, gains, tower_w):
    width = txn_feats.shape[1]
    slots = seg_row.shape[1]
    cap = slots // (X * Y)
    gathered = lax.all_gather(tower_w[0], ("x", "y", "c"), axis=0, tiled=False)
    gain = lax.all_gather(gains[0], "c", axis=0, tiled=False)
    buffer = pool(send_counts, txn_seg, seg_row, txn_feats)
    got = lax.all_to_all(buffer.reshape(X, Y * cap, width + LANES), "x", 0, 0, tiled=True)
    dense = pick(got, cap, Y)
    shares = lax.all_to_all(dense, "y", 0, 0, tiled=True)
    pooled = jnp.sum(shares.astype(jnp.float32), axis=0).astype(jnp.bfloat16)
    weight = load_weights(gathered.reshape(X * Y, C, *tower_w.shape[1:]))
    position = lax.axis_index("z").reshape(1)
    x = pooled
    for step in range(2 * Z):
        if step < 2 * Z - 1:
            x = stage(position, x, gain, weight, step)
        x = lax.ppermute(x, "z", [(i, (i + 1) % Z) for i in range(Z)])
    return x


def solution(mesh):
    split = Mesh(mesh.devices.reshape(X, Y, Z, C), DEVICES)
    in_specs = (
        P(DEVICES, None),
        P(DEVICES, None),
        P(DEVICES, None),
        P(DEVICES, None),
        P(("z", "c"), None),
        P(("z", "c"), ("x", "y"), None),
    )
    return jax.shard_map(
        body, mesh=split, in_specs=in_specs, out_specs=P(DEVICES, None), check_vma=False
    )
```

time: 548 us -> 299 us (0.55)
  the two profiles are of different devices: /device:TPU:1 before, /device:TPU:24 now
where the time goes in v1:
time: 299 us
  waiting for transfers between devices  179 us (60%)
  starting transfers between devices  42.7 us (14%)
  Pallas kernels  31.8 us (11%)
  blocking collectives  21.9 us (7%)
  between operations  13.6 us (5%)
  local copies, waits for them, and re-layouts  9.64 us (3%)
    ppermute x16, waiting for transfers between devices, body(): x = lax.ppermute(x, 'z', [(i, (i + 1) % Z) for i in range(Z)])  96.2 us
    all_gather x1, waiting for transfers between devices, body(): gathered = lax.all_gather(tower_w[0], ('x', 'y', 'c'), axis=0, tiled=False)  66 us
    ppermute x16, starting transfers between devices, body(): x = lax.ppermute(x, 'z', [(i, (i + 1) % Z) for i in range(Z)])  35.4 us
    pallas_call x15, Pallas kernels, stage(): pl.pallas_call(functools.partial(stage_kernel, step=step), out_shape=jax....  28.2 us
    all_to_all x1, blocking collectives, body(): lax.all_to_all(buffer.reshape(X, Y * cap, width + LANES), 'x', 0, 0, tile...  19.9 us
    all_to_all x1, waiting for transfers between devices, body(): shares = lax.all_to_all(dense, 'y', 0, 0, tiled=True)  16.1 us
    unnamed x12, local copies, waits for them, and re-layouts  9.64 us
    all_to_all x1, starting transfers between devices, body(): shares = lax.all_to_all(dense, 'y', 0, 0, tiled=True)  7.32 us
  transfers between devices with their start and end apart: 18, of which 18 were waited for; matrix products, arithmetic and copies ran while one was open for 0% of the time, Pallas kernels for 1%

profile of v1, /device:TPU:24, one launch (start us, length us, event | category | flops | bytes accessed | tf_op | source)
XLA Modules:
  0.0 298.7 jit_solution(2954580870742465423)
XLA Ops:
  11.1 19.9 %all_to_all.10.got_ref = bf16[4,64,2176]{2,1,0:T(8,128)(2,1)S(1)} all-to-all(bf16[4,64,2176]{2,1,0:T(8,128)(2,1)S(1)} %bitcast.9), channel_id=1, replica_groups=mesh['x'=4,'y'=8,'z'=8,'c'=2] {'x'}, dimensions={0} | all-to-all | bytes 2228224 | tf_op jit(solution)/shard_map/all_to_all | solution.py:178
  32.2 7.3 %all-to-all-start.1 = ((bf16[8,16,2048]{2,1,0:T(8,128)(2,1)}), bf16[8,16,2048]{2,1,0:T(8,128)(2,1)S(1)}, u32[]{:S(2)}, u32[]{:S(2)}) async-start(bf16[8,16,2048]{2,1,0:T(8,128)(2,1)} %bitcast.2), calls=%async_computation.1 | async-start | bytes 1048576 | tf_op jit(solution)/shard_map/all_to_all | solution.py:180
  41.6 16.1 %all-to-all-done.1 = bf16[8,16,2048]{2,1,0:T(8,128)(2,1)S(1)} async-done(((bf16[8,16,2048]{2,1,0:T(8,128)(2,1)}), bf16[8,16,2048]{2,1,0:T(8,128)(2,1)S(1)}, u32[]{:S(2)}, u32[]{:S(2)}) %all-to-all-start.1) | async-done | bytes 524320 | tf_op jit(solution)/shard_map/all_to_all | solution.py:180
  57.7 66.0 %all-gather.3.cloned.1.call-done = bf16[64,64,2048]{2,1,0:T(8,128)(2,1)} async-done(((bf16[1,64,2048]{2,1,0:T(8,128)(2,1)}), bf16[64,64,2048]{2,1,0:T(8,128)(2,1)}) %all-gather.3.cloned.1.call-update) | async-done | bytes 16777232 | tf_op jit(solution)/shard_map/all_gather | solution.py:175
  123.7 5.8 %copy-done = bf16[64,64,2048]{2,1,0:T(8,128)(2,1)S(1)} copy-done((bf16[64,64,2048]{2,1,0:T(8,128)(2,1)S(1)}, bf16[64,64,2048]{2,1,0:T(8,128)(2,1)}, u32[]{:S(2)}) %copy-start) | copy-done | bytes 16777240
  131.3 3.5 %stage.15 = bf16[16,2048]{1,0:T(8,128)(2,1)S(1)} custom-call(s32[1]{0:T(128)} %bitcast.position_ref, bf16[16,2048]{1,0:T(8,128)(2,1)S(1)} %reduce_sum.12.x_ref, f32[2,2048]{1,0:T(2,128)S(1)} %bitcast.10, bf16[2,2048,2048]{2,1,0:T(8,128)(2,1)S(1)} %load_weights.1.weight_ref), custom_call_target="tpu_custom_call" | custom-call | tf_op jit(solution)/shard_map/stage/pallas_call | solution.py:160
  136.8 5.4 %collective-permute-done.x_ref = bf16[16,2048]{1,0:T(8,128)(2,1)S(1)} collective-permute-done((bf16[16,2048]{1,0:T(8,128)(2,1)S(1)}, bf16[16,2048]{1,0:T(8,128)(2,1)S(1)}, u32[]{:S(2)}, u32[]{:S(2)}) %collective-permute-start) | collective-permute-done | bytes 65568 | tf_op jit(solution)/shard_map/ppermute | solution.py:188
  142.2 3.5 %stage.16 = bf16[16,2048]{1,0:T(8,128)(2,1)S(1)} custom-call(s32[1]{0:T(128)} %bitcast.position_ref, bf16[16,2048]{1,0:T(8,128)(2,1)S(1)} %collective-permute-done.x_ref, f32[2,2048]{1,0:T(2,128)S(1)} %bitcast.11, bf16[2,2048,2048]{2,1,0:T(8,128)(2,1)S(1)} %load_weights.1.weight_ref), custom_call_target="tpu_custom_call" | custom-call | tf_op jit(solution)/shard_map/stage/pallas_call | solution.py:160
  147.7 5.4 %collective-permute-done.1.x_ref = bf16[16,2048]{1,0:T(8,128)(2,1)S(1)} collective-permute-done((bf16[16,2048]{1,0:T(8,128)(2,1)S(1)}, bf16[16,2048]{1,0:T(8,128)(2,1)S(1)}, u32[]{:S(2)}, u32[]{:S(2)}) %collective-permute-start.1) | collective-permute-done | bytes 65568 | tf_op jit(solution)/shard_map/ppermute | solution.py:188
  158.6 5.4 %collective-permute-done.2.x_ref = bf16[16,2048]{1,0:T(8,128)(2,1)S(1)} collective-permute-done((bf16[16,2048]{1,0:T(8,128)(2,1)S(1)}, bf16[16,2048]{1,0:T(8,128)(2,1)S(1)}, u32[]{:S(2)}, u32[]{:S(2)}) %collective-permute-start.2) | collective-permute-done | bytes 65568 | tf_op jit(solution)/shard_map/ppermute | solution.py:188
  169.5 5.4 %collective-permute-done.3.x_ref = bf16[16,2048]{1,0:T(8,128)(2,1)S(1)} collective-permute-done((bf16[16,2048]{1,0:T(8,128)(2,1)S(1)}, bf16[16,2048]{1,0:T(8,128)(2,1)S(1)}, u32[]{:S(2)}, u32[]{:S(2)}) %collective-permute-start.3) | collective-permute-done | bytes 65568 | tf_op jit(solution)/shard_map/ppermute | solution.py:188
  180.3 5.4 %collective-permute-done.4.x_ref = bf16[16,2048]{1,0:T(8,128)(2,1)S(1)} collective-permute-done((bf16[16,2048]{1,0:T(8,128)(2,1)S(1)}, bf16[16,2048]{1,0:T(8,128)(2,1)S(1)}, u32[]{:S(2)}, u32[]{:S(2)}) %collective-permute-start.4) | collective-permute-done | bytes 65568 | tf_op jit(solution)/shard_map/ppermute | solution.py:188
  191.2 5.4 %collective-permute-done.5.x_ref = bf16[16,2048]{1,0:T(8,128)(2,1)S(1)} collective-permute-done((bf16[16,2048]{1,0:T(8,128)(2,1)S(1)}, bf16[16,2048]{1,0:T(8,128)(2,1)S(1)}, u32[]{:S(2)}, u32[]{:S(2)}) %collective-permute-start.5) | collective-permute-done | bytes 65568 | tf_op jit(solution)/shard_map/ppermute | solution.py:188
  202.1 5.4 %collective-permute-done.6.x_ref = bf16[16,2048]{1,0:T(8,128)(2,1)S(1)} collective-permute-done((bf16[16,2048]{1,0:T(8,128)(2,1)S(1)}, bf16[16,2048]{1,0:T(8,128)(2,1)S(1)}, u32[]{:S(2)}, u32[]{:S(2)}) %collective-permute-start.6) | collective-permute-done | bytes 65568 | tf_op jit(solution)/shard_map/ppermute | solution.py:188
  213.0 5.4 %collective-permute-done.7.x_ref = bf16[16,2048]{1,0:T(8,128)(2,1)S(1)} collective-permute-done((bf16[16,2048]{1,0:T(8,128)(2,1)S(1)}, bf16[16,2048]{1,0:T(8,128)(2,1)S(1)}, u32[]{:S(2)}, u32[]{:S(2)}) %collective-permute-start.7) | collective-permute-done | bytes 65568 | tf_op jit(solution)/shard_map/ppermute | solution.py:188
  218.5 4.9 %collective-permute-start.8 = (bf16[16,2048]{1,0:T(8,128)(2,1)S(1)}, bf16[16,2048]{1,0:T(8,128)(2,1)S(1)}, u32[]{:S(2)}, u32[]{:S(2)}) collective-permute-start(bf16[16,2048]{1,0:T(8,128)(2,1)S(1)} %stage.23), channel_id=1, source_target_pairs={{0,2},{2,4},{4,6},{6,8},{8,10},{10,12},{12,14},{14,0},{1,3},{3,5},... | collective-permute-start | bytes 196616 | tf_op jit(solution)/shard_map/ppermute | solution.py:188
  225.8 3.7 %collective-permute-start.9 = (bf16[16,2048]{1,0:T(8,128)(2,1)S(1)}, bf16[16,2048]{1,0:T(8,128)(2,1)S(1)}, u32[]{:S(2)}, u32[]{:S(2)}) collective-permute-start(bf16[16,2048]{1,0:T(8,128)(2,1)S(1)} %stage.24), channel_id=1, source_target_pairs={{0,2},{2,4},{4,6},{6,8},{8,10},{10,12},{12,14},{14,0},{1,3},{3,5},... | collective-permute-start | bytes 196616 | tf_op jit(solution)/shard_map/ppermute | solution.py:188
  229.5 6.0 %collective-permute-done.9.x_ref = bf16[16,2048]{1,0:T(8,128)(2,1)S(1)} collective-permute-done((bf16[16,2048]{1,0:T(8,128)(2,1)S(1)}, bf16[16,2048]{1,0:T(8,128)(2,1)S(1)}, u32[]{:S(2)}, u32[]{:S(2)}) %collective-permute-start.9) | collective-permute-done | bytes 65568 | tf_op jit(solution)/shard_map/ppermute | solution.py:188
  237.4 7.8 %collective-permute-done.10.x_ref = bf16[16,2048]{1,0:T(8,128)(2,1)S(1)} collective-permute-done((bf16[16,2048]{1,0:T(8,128)(2,1)S(1)}, bf16[16,2048]{1,0:T(8,128)(2,1)S(1)}, u32[]{:S(2)}, u32[]{:S(2)}) %collective-permute-start.10) | collective-permute-done | bytes 65568 | tf_op jit(solution)/shard_map/ppermute | solution.py:188
  247.1 7.8 %collective-permute-done.11.x_ref = bf16[16,2048]{1,0:T(8,128)(2,1)S(1)} collective-permute-done((bf16[16,2048]{1,0:T(8,128)(2,1)S(1)}, bf16[16,2048]{1,0:T(8,128)(2,1)S(1)}, u32[]{:S(2)}, u32[]{:S(2)}) %collective-permute-start.11) | collective-permute-done | bytes 65568 | tf_op jit(solution)/shard_map/ppermute | solution.py:188
  256.8 7.8 %collective-permute-done.12.x_ref = bf16[16,2048]{1,0:T(8,128)(2,1)S(1)} collective-permute-done((bf16[16,2048]{1,0:T(8,128)(2,1)S(1)}, bf16[16,2048]{1,0:T(8,128)(2,1)S(1)}, u32[]{:S(2)}, u32[]{:S(2)}) %collective-permute-start.12) | collective-permute-done | bytes 65568 | tf_op jit(solution)/shard_map/ppermute | solution.py:188
  266.4 8.1 %collective-permute-done.13.x_ref = bf16[16,2048]{1,0:T(8,128)(2,1)S(1)} collective-permute-done((bf16[16,2048]{1,0:T(8,128)(2,1)S(1)}, bf16[16,2048]{1,0:T(8,128)(2,1)S(1)}, u32[]{:S(2)}, u32[]{:S(2)}) %collective-permute-start.13) | collective-permute-done | bytes 65568 | tf_op jit(solution)/shard_map/ppermute | solution.py:188
  276.5 7.4 %collective-permute-done.14 = bf16[16,2048]{1,0:T(8,128)(2,1)S(1)} collective-permute-done((bf16[16,2048]{1,0:T(8,128)(2,1)S(1)}, bf16[16,2048]{1,0:T(8,128)(2,1)S(1)}, u32[]{:S(2)}, u32[]{:S(2)}) %collective-permute-start.14) | collective-permute-done | bytes 65568 | tf_op jit(solution)/shard_map/ppermute | solution.py:188
  285.8 5.4 %collective-permute-done.15 = bf16[16,2048]{1,0:T(8,128)(2,1)S(1)} collective-permute-done((bf16[16,2048]{1,0:T(8,128)(2,1)S(1)}, bf16[16,2048]{1,0:T(8,128)(2,1)S(1)}, u32[]{:S(2)}, u32[]{:S(2)}) %collective-permute-start.15) | collective-permute-done | bytes 65568 | tf_op jit(solution)/shard_map/ppermute | solution.py:188
  (46 shorter events, 60.7 us)
Async XLA Ops:
  6.5 117.2 %all-gather.3.cloned.1.call-start = ((), (), s32[]{:S(2)}) async-start(), calls=%async_computation.2 | async-start | bytes 17039360 | tf_op jit(solution)/shard_map/all_gather | solution.py:175
  7.3 1.2 copy-start.1
  8.5 0.7 copy-start.2
  9.2 0.7 copy-start.3
  9.8 0.7 copy-start.4
  32.2 25.5 %all-to-all-start.1 = ((bf16[8,16,2048]{2,1,0:T(8,128)(2,1)}), bf16[8,16,2048]{2,1,0:T(8,128)(2,1)S(1)}, u32[]{:S(2)}, u32[]{:S(2)}) async-start(bf16[8,16,2048]{2,1,0:T(8,128)(2,1)} %bitcast.2), calls=%async_computation.1 | async-start | bytes 1048576 | tf_op jit(solution)/shard_map/all_to_all | solution.py:180
  123.7 5.8 %copy-start = (bf16[64,64,2048]{2,1,0:T(8,128)(2,1)S(1)}, bf16[64,64,2048]{2,1,0:T(8,128)(2,1)}, u32[]{:S(2)}) copy-start(bf16[64,64,2048]{2,1,0:T(8,128)(2,1)} %all-gather.3.cloned.1.call-done) | copy-start | bytes 50331652
  134.8 7.4 %collective-permute-start = (bf16[16,2048]{1,0:T(8,128)(2,1)S(1)}, bf16[16,2048]{1,0:T(8,128)(2,1)S(1)}, u32[]{:S(2)}, u32[]{:S(2)}) collective-permute-start(bf16[16,2048]{1,0:T(8,128)(2,1)S(1)} %stage.15), channel_id=1, source_target_pairs={{0,2},{2,4},{4,6},{6,8},{8,10},{10,12},{12,14},{14,0},{1,3},{3,5},... | collective-permute-start | bytes 196616 | tf_op jit(solution)/shard_map/ppermute | solution.py:188
  145.7 7.4 %collective-permute-start.1 = (bf16[16,2048]{1,0:T(8,128)(2,1)S(1)}, bf16[16,2048]{1,0:T(8,128)(2,1)S(1)}, u32[]{:S(2)}, u32[]{:S(2)}) collective-permute-start(bf16[16,2048]{1,0:T(8,128)(2,1)S(1)} %stage.16), channel_id=1, source_target_pairs={{0,2},{2,4},{4,6},{6,8},{8,10},{10,12},{12,14},{14,0},{1,3},{3,5},... | collective-permute-start | bytes 196616 | tf_op jit(solution)/shard_map/ppermute | solution.py:188
  156.6 7.4 %collective-permute-start.2 = (bf16[16,2048]{1,0:T(8,128)(2,1)S(1)}, bf16[16,2048]{1,0:T(8,128)(2,1)S(1)}, u32[]{:S(2)}, u32[]{:S(2)}) collective-permute-start(bf16[16,2048]{1,0:T(8,128)(2,1)S(1)} %stage.17), channel_id=1, source_target_pairs={{0,2},{2,4},{4,6},{6,8},{8,10},{10,12},{12,14},{14,0},{1,3},{3,5},... | collective-permute-start | bytes 196616 | tf_op jit(solution)/shard_map/ppermute | solution.py:188
  167.5 7.4 %collective-permute-start.3 = (bf16[16,2048]{1,0:T(8,128)(2,1)S(1)}, bf16[16,2048]{1,0:T(8,128)(2,1)S(1)}, u32[]{:S(2)}, u32[]{:S(2)}) collective-permute-start(bf16[16,2048]{1,0:T(8,128)(2,1)S(1)} %stage.18), channel_id=1, source_target_pairs={{0,2},{2,4},{4,6},{6,8},{8,10},{10,12},{12,14},{14,0},{1,3},{3,5},... | collective-permute-start | bytes 196616 | tf_op jit(solution)/shard_map/ppermute | solution.py:188
  178.4 7.4 %collective-permute-start.4 = (bf16[16,2048]{1,0:T(8,128)(2,1)S(1)}, bf16[16,2048]{1,0:T(8,128)(2,1)S(1)}, u32[]{:S(2)}, u32[]{:S(2)}) collective-permute-start(bf16[16,2048]{1,0:T(8,128)(2,1)S(1)} %stage.19), channel_id=1, source_target_pairs={{0,2},{2,4},{4,6},{6,8},{8,10},{10,12},{12,14},{14,0},{1,3},{3,5},... | collective-permute-start | bytes 196616 | tf_op jit(solution)/shard_map/ppermute | solution.py:188
  189.3 7.4 %collective-permute-start.5 = (bf16[16,2048]{1,0:T(8,128)(2,1)S(1)}, bf16[16,2048]{1,0:T(8,128)(2,1)S(1)}, u32[]{:S(2)}, u32[]{:S(2)}) collective-permute-start(bf16[16,2048]{1,0:T(8,128)(2,1)S(1)} %stage.20), channel_id=1, source_target_pairs={{0,2},{2,4},{4,6},{6,8},{8,10},{10,12},{12,14},{14,0},{1,3},{3,5},... | collective-permute-start | bytes 196616 | tf_op jit(solution)/shard_map/ppermute | solution.py:188
  200.2 7.4 %collective-permute-start.6 = (bf16[16,2048]{1,0:T(8,128)(2,1)S(1)}, bf16[16,2048]{1,0:T(8,128)(2,1)S(1)}, u32[]{:S(2)}, u32[]{:S(2)}) collective-permute-start(bf16[16,2048]{1,0:T(8,128)(2,1)S(1)} %stage.21), channel_id=1, source_target_pairs={{0,2},{2,4},{4,6},{6,8},{8,10},{10,12},{12,14},{14,0},{1,3},{3,5},... | collective-permute-start | bytes 196616 | tf_op jit(solution)/shard_map/ppermute | solution.py:188
  211.1 7.4 %collective-permute-start.7 = (bf16[16,2048]{1,0:T(8,128)(2,1)S(1)}, bf16[16,2048]{1,0:T(8,128)(2,1)S(1)}, u32[]{:S(2)}, u32[]{:S(2)}) collective-permute-start(bf16[16,2048]{1,0:T(8,128)(2,1)S(1)} %stage.22), channel_id=1, source_target_pairs={{0,2},{2,4},{4,6},{6,8},{8,10},{10,12},{12,14},{14,0},{1,3},{3,5},... | collective-permute-start | bytes 196616 | tf_op jit(solution)/shard_map/ppermute | solution.py:188
  218.5 7.4 %collective-permute-start.8 = (bf16[16,2048]{1,0:T(8,128)(2,1)S(1)}, bf16[16,2048]{1,0:T(8,128)(2,1)S(1)}, u32[]{:S(2)}, u32[]{:S(2)}) collective-permute-start(bf16[16,2048]{1,0:T(8,128)(2,1)S(1)} %stage.23), channel_id=1, source_target_pairs={{0,2},{2,4},{4,6},{6,8},{8,10},{10,12},{12,14},{14,0},{1,3},{3,5},... | collective-permute-start | bytes 196616 | tf_op jit(solution)/shard_map/ppermute | solution.py:188
  225.8 9.6 %collective-permute-start.9 = (bf16[16,2048]{1,0:T(8,128)(2,1)S(1)}, bf16[16,2048]{1,0:T(8,128)(2,1)S(1)}, u32[]{:S(2)}, u32[]{:S(2)}) collective-permute-start(bf16[16,2048]{1,0:T(8,128)(2,1)S(1)} %stage.24), channel_id=1, source_target_pairs={{0,2},{2,4},{4,6},{6,8},{8,10},{10,12},{12,14},{14,0},{1,3},{3,5},... | collective-permute-start | bytes 196616 | tf_op jit(solution)/shard_map/ppermute | solution.py:188
  235.5 9.7 %collective-permute-start.10 = (bf16[16,2048]{1,0:T(8,128)(2,1)S(1)}, bf16[16,2048]{1,0:T(8,128)(2,1)S(1)}, u32[]{:S(2)}, u32[]{:S(2)}) collective-permute-start(bf16[16,2048]{1,0:T(8,128)(2,1)S(1)} %stage.25), channel_id=1, source_target_pairs={{0,2},{2,4},{4,6},{6,8},{8,10},{10,12},{12,14},{14,0},{1,3},{3,5},... | collective-permute-start | bytes 196616 | tf_op jit(solution)/shard_map/ppermute | solution.py:188
  245.2 9.7 %collective-permute-start.11 = (bf16[16,2048]{1,0:T(8,128)(2,1)S(1)}, bf16[16,2048]{1,0:T(8,128)(2,1)S(1)}, u32[]{:S(2)}, u32[]{:S(2)}) collective-permute-start(bf16[16,2048]{1,0:T(8,128)(2,1)S(1)} %stage.26), channel_id=1, source_target_pairs={{0,2},{2,4},{4,6},{6,8},{8,10},{10,12},{12,14},{14,0},{1,3},{3,5},... | collective-permute-start | bytes 196616 | tf_op jit(solution)/shard_map/ppermute | solution.py:188
  254.8 9.7 %collective-permute-start.12 = (bf16[16,2048]{1,0:T(8,128)(2,1)S(1)}, bf16[16,2048]{1,0:T(8,128)(2,1)S(1)}, u32[]{:S(2)}, u32[]{:S(2)}) collective-permute-start(bf16[16,2048]{1,0:T(8,128)(2,1)S(1)} %stage.27), channel_id=1, source_target_pairs={{0,2},{2,4},{4,6},{6,8},{8,10},{10,12},{12,14},{14,0},{1,3},{3,5},... | collective-permute-start | bytes 196616 | tf_op jit(solution)/shard_map/ppermute | solution.py:188
  264.5 10.0 %collective-permute-start.13 = (bf16[16,2048]{1,0:T(8,128)(2,1)S(1)}, bf16[16,2048]{1,0:T(8,128)(2,1)S(1)}, u32[]{:S(2)}, u32[]{:S(2)}) collective-permute-start(bf16[16,2048]{1,0:T(8,128)(2,1)S(1)} %stage.28), channel_id=1, source_target_pairs={{0,2},{2,4},{4,6},{6,8},{8,10},{10,12},{12,14},{14,0},{1,3},{3,5},... | collective-permute-start | bytes 196616 | tf_op jit(solution)/shard_map/ppermute | solution.py:188
  274.6 9.3 %collective-permute-start.14 = (bf16[16,2048]{1,0:T(8,128)(2,1)S(1)}, bf16[16,2048]{1,0:T(8,128)(2,1)S(1)}, u32[]{:S(2)}, u32[]{:S(2)}) collective-permute-start(bf16[16,2048]{1,0:T(8,128)(2,1)S(1)} %stage.29), channel_id=1, source_target_pairs={{0,2},{2,4},{4,6},{6,8},{8,10},{10,12},{12,14},{14,0},{1,3},{3,5},... | collective-permute-start | bytes 196616 | tf_op jit(solution)/shard_map/ppermute | solution.py:188
  283.9 7.4 %collective-permute-start.15 = (bf16[16,2048]{1,0:T(8,128)(2,1)S(1)}, bf16[16,2048]{1,0:T(8,128)(2,1)S(1)}, u32[]{:S(2)}, u32[]{:S(2)}) collective-permute-start(bf16[16,2048]{1,0:T(8,128)(2,1)S(1)} %collective-permute-done.14), channel_id=1, source_target_pairs={{0,2},{2,4},{4,6},{6,8},{8,10},{10,12},{12,14},{14,0},{1,3},{3,5},... | collective-permute-start | bytes 196616 | tf_op jit(solution)/shard_map/ppermute | solution.py:188
Sparse Core Ops, SparseCore 0:
  10.7 112.9 all-gather.2

commit v2 on v1

--- a/solution.py
+++ b/solution.py
@@ -11,7 +11,9 @@
 X, Y, Z, C = 4, 8, 8, 2
 DEVICES = ("x", "y", "z", "c")
 LANES = 128
-BLOCK = 512
+BLOCK = 1024
+TURNS = 2
+BATCH = 2 * CARD_DEV
 VMEM = pltpu.MemorySpace.VMEM
 SMEM = pltpu.MemorySpace.SMEM
 MIB = 1024 * 1024
@@ -119,7 +121,7 @@
     return pl.pallas_call(
         load_kernel,
         out_shape=pltpu.VMEM((layers, blocks * rows, width), jnp.bfloat16),
-        in_specs=[pl.BlockSpec(memory_space=pl.ANY)],
+        in_specs=[pl.BlockSpec(memory_space=pltpu.MemorySpace.HBM)],
         out_specs=pl.BlockSpec(memory_space=VMEM),
         scratch_shapes=[pltpu.SemaphoreType.DMA((blocks, layers))],
         compiler_params=pltpu.CompilerParams(vmem_limit_bytes=20 * MIB),
@@ -127,45 +129,130 @@
     )(gathered)
 
 
-def stage_kernel(position_ref, x_ref, gain_ref, weight_ref, out_ref, normed_ref, *, step):
-    active = (step >= position_ref[0]) & (step < position_ref[0] + Z)
-    width = x_ref.shape[1]
-    out_ref[...] = x_ref[...]
-
-    @pl.when(active)
+def run_layers(out_ref, gain_ref, weight_ref, normed_ref):
+    width = out_ref.shape[1]
+
+    def layer_of(layer, carry):
+        u = out_ref[...].astype(jnp.float32)
+        mean_sq = jnp.mean(u * u, axis=-1, keepdims=True)
+        normed = u * lax.rsqrt(mean_sq + 1e-05) * gain_ref[pl.ds(layer, 1), :]
+        normed_ref[...] = normed.astype(jnp.bfloat16)
+
+        def columns_of(block, carry):
+            columns = pl.ds(pl.multiple_of(block * BLOCK, BLOCK), BLOCK)
+            y = jnp.dot(
+                normed_ref[...],
+                weight_ref[layer, :, columns],
+                preferred_element_type=jnp.float32,
+            )
+            u = out_ref[:, columns].astype(jnp.float32)
+            out_ref[:, columns] = (u + y / (1.0 + jnp.exp(-y))).astype(jnp.bfloat16)
+            return carry
+
+        return lax.fori_loop(0, width // BLOCK, columns_of, carry)
+
+    lax.fori_loop(0, weight_ref.shape[0], layer_of, 0)
+
+
+def stage_kernel(position_ref, *refs, step, fresh):
+    *sources, gain_ref, weight_ref, out_ref, normed_ref = refs
+    age = step - position_ref[0]
+
+    @pl.when((age >= 0) & (age < TURNS))
     def _():
-        def layer_of(layer, carry):
-            u = out_ref[...].astype(jnp.float32)
-            mean_sq = jnp.mean(u * u, axis=-1, keepdims=True)
-            normed = u * lax.rsqrt(mean_sq + 1e-05) * gain_ref[pl.ds(layer, 1), :]
-            normed_ref[...] = normed.astype(jnp.bfloat16)
-
-            def columns_of(block, carry):
-                columns = pl.ds(pl.multiple_of(block * BLOCK, BLOCK), BLOCK)
-                y = jnp.dot(
-                    normed_ref[...],
-                    weight_ref[layer, :, columns],
-                    preferred_element_type=jnp.float32,
-                )
-                u = out_ref[:, columns].astype(jnp.float32)
-                out_ref[:, columns] = (u + y / (1.0 + jnp.exp(-y))).astype(jnp.bfloat16)
-                return carry
-
-            return lax.fori_loop(0, width // BLOCK, columns_of, carry)
-
-        lax.fori_loop(0, weight_ref.shape[0], layer_of, 0)
-
-
-def stage(position, x, gain, weight, step):
-    return pl.pallas_call(
-        functools.partial(stage_kernel, step=step),
-        out_shape=jax.ShapeDtypeStruct(x.shape, x.dtype),
-        in_specs=[pl.BlockSpec(memory_space=SMEM)] + [pl.BlockSpec(memory_space=VMEM)] * 3,
-        out_specs=pl.BlockSpec(memory_space=VMEM),
-        scratch_shapes=[pltpu.VMEM(x.shape, jnp.bfloat16)],
+        if fresh is None:
+            out_ref[...] = sources[-1][...]
+        elif len(sources) == 1:
+            out_ref[...] = sources[0][fresh : fresh + BATCH, :]
+        else:
+            first = position_ref[0] == 0
+
+            @pl.when(first)
+            def _():
+                out_ref[...] = sources[0][fresh : fresh + BATCH, :]
+
+            @pl.when(jnp.logical_not(first))
+            def _():
+                out_ref[...] = sources[1][...]
+
+        run_layers(out_ref, gain_ref, weight_ref, normed_ref)
+
+
+def stage(position, queue, came, gain, weight, step, fresh):
+    sources = [a for a in (queue if fresh is not None else None, came) if a is not None]
+    shape = (BATCH, gain.shape[1])
+    return pl.pallas_call(
+        functools.partial(stage_kernel, step=step, fresh=fresh),
+        out_shape=jax.ShapeDtypeStruct(shape, jnp.bfloat16),
+        in_specs=[pl.BlockSpec(memory_space=SMEM)]
+        + [pl.BlockSpec(memory_space=VMEM)] * (len(sources) + 2),
+        out_specs=pl.BlockSpec(memory_space=VMEM),
+        scratch_shapes=[pltpu.VMEM(shape, jnp.bfloat16)],
         compiler_params=pltpu.CompilerParams(vmem_limit_bytes=24 * MIB),
         name="stage",
-    )(position, x, gain, weight)
+    )(position, *sources, gain, weight)
+
+
+def choose_kernel(position_ref, *refs, cases):
+    out_ref = refs[-1]
+    for homes, which, row in cases:
+        mine = position_ref[0] == homes[0]
+        for home in homes[1:]:
+            mine = mine | (position_ref[0] == home)
+
+        @pl.when(mine)
+        def _():
+            out_ref[...] = refs[which][row : row + CARD_DEV, :]
+
+
+def choose(position, arrays, cases):
+    return pl.pallas_call(
+        functools.partial(choose_kernel, cases=cases),
+        out_shape=jax.ShapeDtypeStruct((CARD_DEV, arrays[0].shape[1]), jnp.bfloat16),
+        in_specs=[pl.BlockSpec(memory_space=SMEM)]
+        + [pl.BlockSpec(memory_space=VMEM)] * len(arrays),
+        out_specs=pl.BlockSpec(memory_space=VMEM),
+        compiler_params=pltpu.CompilerParams(vmem_limit_bytes=8 * MIB),
+        name="choose",
+    )(position, *arrays)
+
+
+def collect(pooled):
+    pairs = jnp.concatenate([lax.ppermute(pooled, "z", [(7, 0), (1, 2), (3, 4), (5, 6)]), pooled])
+    fours = jnp.concatenate([pairs, lax.ppermute(pairs, "z", [(2, 0), (6, 4)])])
+    return jnp.concatenate([fours, lax.ppermute(fours, "z", [(4, 0)])])
+
+
+def tower(position, queue, gain, weight):
+    streams = [
+        dict(fresh=(2 * CARD_DEV, 6 * CARD_DEV), home=(2, 6)),
+        dict(fresh=(4 * CARD_DEV, 0), home=(4, 0)),
+    ]
+    came = [None, None]
+    kept = [[], []]
+    done = [None, None]
+    for step in range(Z - 1 + TURNS):
+        for s, stream in enumerate(streams):
+            fresh = stream["fresh"][step] if step < TURNS else None
+            done[s] = stage(position, queue, came[s], gain, weight, step, fresh)
+            moves = [(z, z + 1) for z in range(Z - 1) if 0 <= step - z < TURNS]
+            if step >= Z - 1:
+                moves.append((Z - 1, stream["home"][step - Z + 1]))
+            came[s] = lax.ppermute(done[s], "z", moves)
+            if step >= Z - 1:
+                kept[s].append(came[s])
+    (two, six), (four, zero) = kept
+    lent = choose(position, [two, four, six], (((2,), 0, 0), ((4,), 1, 0), ((6,), 2, 0)))
+    lent = lax.ppermute(lent, "z", [(2, 1), (4, 3), (6, 5)])
+    cases = (
+        ((2,), 0, CARD_DEV),
+        ((4,), 1, CARD_DEV),
+        ((6,), 2, CARD_DEV),
+        ((0,), 3, CARD_DEV),
+        ((1, 3, 5), 4, 0),
+        ((7,), 5, 0),
+    )
+    return choose(position, [two, four, six, zero, lent, done[1]], cases)
 
 
 def body(txn_feats, txn_seg, seg_row, send_counts, gains, tower_w):
@@ -179,14 +266,10 @@
     dense = pick(got, cap, Y)
     shares = lax.all_to_all(dense, "y", 0, 0, tiled=True)
     pooled = jnp.sum(shares.astype(jnp.float32), axis=0).astype(jnp.bfloat16)
+    queue = collect(pooled)
     weight = load_weights(gathered.reshape(X * Y, C, *tower_w.shape[1:]))
     position = lax.axis_index("z").reshape(1)
-    x = pooled
-    for step in range(2 * Z):
-        if step < 2 * Z - 1:
-            x = stage(position, x, gain, weight, step)
-        x = lax.ppermute(x, "z", [(i, (i + 1) % Z) for i in range(Z)])
-    return x
+    return tower(position, queue, gain, weight)
 
 
 def solution(mesh):

time: 299 us -> 235 us (0.79)
  waiting for transfers between devices: 179 us -> 125 us
  blocking collectives: 21.9 us -> 46.6 us
  starting transfers between devices: 42.7 us -> 21.8 us
  Pallas kernels: 31.8 us -> 18.7 us
    all_gather x1, waiting for transfers between devices: 66 us -> 35.4 us  [body(): gathered = lax.all_gather(tower_w[0], ('x', 'y', 'c'), axis=0, tiled=False)]
    all_to_all x0 -> x1, blocking collectives: none -> 24.7 us  [body(): shares = lax.all_to_all(dense, 'y', 0, 0, tiled=True)]
    all_to_all x1 -> x0, waiting for transfers between devices: 16.1 us -> none  [body(): shares = lax.all_to_all(dense, 'y', 0, 0, tiled=True)]
    ppermute x16 -> x22, starting transfers between devices: 35.4 us -> 21.8 us  [the longest x18 17.3 us: tower(): came[s] = lax.ppermute(done[s], 'z', moves)]
    pallas_call x15 -> x20, Pallas kernels: 28.2 us -> 15.9 us  [the longest x18 15.2 us: stage(): pl.pallas_call(functools.partial(stage_kernel, step=step, fresh=fresh), o...]
    ppermute x16 -> x22, waiting for transfers between devices: 96.2 us -> 88.6 us  [the longest x18 62.1 us: tower(): came[s] = lax.ppermute(done[s], 'z', moves)]
    all_to_all x1 -> x0, starting transfers between devices: 7.32 us -> none  [body(): shares = lax.all_to_all(dense, 'y', 0, 0, tiled=True)]
    unnamed x12 -> x11, local copies, waits for them, and re-layouts: 9.64 us -> 9.01 us
  transfers between devices with their start and end apart: 18 -> 23, of which waited for: 18 -> 6; matrix products, arithmetic and copies ran while one was open for 0% -> 0% of each run, Pallas kernels for 1% -> 5%
where the time goes in v2:
time: 235 us
  waiting for transfers between devices  125 us (53%)
  blocking collectives  46.6 us (20%)
  starting transfers between devices  21.8 us (9%)
  Pallas kernels  18.7 us (8%)
  between operations  13.9 us (6%)
  local copies, waits for them, and re-layouts  9.01 us (4%)
    ppermute x18, waiting for transfers between devices, tower(): came[s] = lax.ppermute(done[s], 'z', moves)  62.1 us
    all_gather x1, waiting for transfers between devices, body(): gathered = lax.all_gather(tower_w[0], ('x', 'y', 'c'), axis=0, tiled=False)  35.4 us
    all_to_all x1, blocking collectives, body(): shares = lax.all_to_all(dense, 'y', 0, 0, tiled=True)  24.7 us
    all_to_all x1, blocking collectives, body(): lax.all_to_all(buffer.reshape(X, Y * cap, width + LANES), 'x', 0, 0, tile...  19.9 us
    ppermute x18, starting transfers between devices, tower(): came[s] = lax.ppermute(done[s], 'z', moves)  17.3 us
    pallas_call x18, Pallas kernels, stage(): pl.pallas_call(functools.partial(stage_kernel, step=step, fresh=fresh), o...  15.2 us
    ppermute x1, waiting for transfers between devices, collect(): lax.ppermute(pooled, 'z', [(7, 0), (1, 2), (3, 4), (5, 6)])  11.1 us
    unnamed x11, local copies, waits for them, and re-layouts  9.01 us
  transfers between devices with their start and end apart: 23, of which 6 were waited for; matrix products, arithmetic and copies ran while one was open for 0% of the time, Pallas kernels for 5%

profile of v2, /device:TPU:24, one launch (start us, length us, event | category | flops | bytes accessed | tf_op | source)
XLA Modules:
  0.0 234.9 jit_solution(16834253609969052742)
XLA Ops:
  7.3 1.2 copy-done.1
  11.1 19.9 %all_to_all.10.got_ref = bf16[4,64,2176]{2,1,0:T(8,128)(2,1)S(1)} all-to-all(bf16[4,64,2176]{2,1,0:T(8,128)(2,1)S(1)} %bitcast.27), channel_id=1, replica_groups=mesh['x'=4,'y'=8,'z'=8,'c'=2] {'x'}, dimensions={0} | all-to-all | bytes 2228224 | tf_op jit(solution)/shard_map/all_to_all | solution.py:265
  31.4 24.7 %all_to_all.11 = bf16[8,16,2048]{2,1,0:T(8,128)(2,1)S(1)} all-to-all(bf16[8,16,2048]{2,1,0:T(8,128)(2,1)S(1)} %bitcast.28), channel_id=1, replica_groups=mesh['x'=4,'y'=8,'z'=8,'c'=2] {'y'}, dimensions={0} | all-to-all | bytes 1048576 | tf_op jit(solution)/shard_map/all_to_all | solution.py:267
  56.2 1.3 collective-permute-start
  57.5 11.1 %collective-permute-done = bf16[16,2048]{1,0:T(8,128)(2,1)S(1)} collective-permute-done((bf16[16,2048]{1,0:T(8,128)(2,1)S(1)}, bf16[16,2048]{1,0:T(8,128)(2,1)S(1)}, u32[]{:S(2)}, u32[]{:S(2)}) %collective-permute-start) | collective-permute-done | bytes 65568 | tf_op jit(solution)/shard_map/ppermute | solution.py:221
  68.6 1.3 collective-permute-start.1
  69.9 6.5 %collective-permute-done.1 = bf16[32,2048]{1,0:T(8,128)(2,1)S(1)} collective-permute-done((bf16[32,2048]{1,0:T(8,128)(2,1)S(1)}, bf16[32,2048]{1,0:T(8,128)(2,1)S(1)}, u32[]{:S(2)}, u32[]{:S(2)}) %collective-permute-start.1) | collective-permute-done | bytes 131104 | tf_op jit(solution)/shard_map/ppermute | solution.py:222
  76.4 1.3 collective-permute-start.2
  77.7 2.0 all-gather
  79.8 8.8 %collective-permute-done.2 = bf16[64,2048]{1,0:T(8,128)(2,1)S(1)} collective-permute-done((bf16[64,2048]{1,0:T(8,128)(2,1)S(1)}, bf16[64,2048]{1,0:T(8,128)(2,1)S(1)}, u32[]{:S(2)}, u32[]{:S(2)}) %collective-permute-start.2) | collective-permute-done | bytes 262176 | tf_op jit(solution)/shard_map/ppermute | solution.py:223
  88.6 35.4 %all-gather.3.cloned.1.call-done = bf16[64,64,2048]{2,1,0:T(8,128)(2,1)} async-done(((bf16[1,64,2048]{2,1,0:T(8,128)(2,1)}), bf16[64,64,2048]{2,1,0:T(8,128)(2,1)}) %all-gather.3.cloned.1.call-update) | async-done | bytes 16777232 | tf_op jit(solution)/shard_map/all_gather | solution.py:262
  124.1 5.8 %copy-done = bf16[64,64,2048]{2,1,0:T(8,128)(2,1)S(1)} copy-done((bf16[64,64,2048]{2,1,0:T(8,128)(2,1)S(1)}, bf16[64,64,2048]{2,1,0:T(8,128)(2,1)}, u32[]{:S(2)}) %copy-start) | copy-done | bytes 16777240
  129.8 1.8 load_weights.1.refs_2_.refs_3_
  131.7 3.7 %stage.18 = bf16[32,2048]{1,0:T(8,128)(2,1)S(1)} custom-call(s32[1]{0:T(128)} %bitcast.position_ref, bf16[128,2048]{1,0:T(8,128)(2,1)S(1)} %pad_maximum_fusion.refs_0_, f32[2,2048]{1,0:T(2,128)S(1)} %bitcast.9, bf16[2,2048,2048]{2,1,0:T(8,128)(2,1)S(1)} %load_weights.1.refs_2_.refs_3_), custom_call_target="tpu_custom_call" | custom-call | tf_op jit(solution)/shard_map/stage/pallas_call | solution.py:184
  135.4 1.3 collective-permute-start.3
  136.7 3.7 %stage.26 = bf16[32,2048]{1,0:T(8,128)(2,1)S(1)} custom-call(s32[1]{0:T(128)} %bitcast.position_ref, bf16[128,2048]{1,0:T(8,128)(2,1)S(1)} %pad_maximum_fusion.refs_0_, f32[2,2048]{1,0:T(2,128)S(1)} %bitcast.10, bf16[2,2048,2048]{2,1,0:T(8,128)(2,1)S(1)} %load_weights.1.refs_2_.refs_3_), custom_call_target="tpu_custom_call" | custom-call | tf_op jit(solution)/shard_map/stage/pallas_call | solution.py:184
  140.4 1.3 collective-permute-start.11
  141.8 3.7 %stage.19 = bf16[32,2048]{1,0:T(8,128)(2,1)S(1)} custom-call(s32[1]{0:T(128)} %bitcast.position_ref, bf16[128,2048]{1,0:T(8,128)(2,1)S(1)} %pad_maximum_fusion.refs_0_, bf16[32,2048]{1,0:T(8,128)(2,1)S(1)} %collective-permute-done.3.refs_1_, f32[2,2048]{1,0:T(2,128)S(1)} %bitcast.11, bf16[2,2048,2048]{2,1,0:T(8,128)(2,1)S(1)} %load_weights.1.refs_2_.refs_3_), custom_call_target="tpu_custom_call" | custom-call | tf_op jit(solution)/shard_map/stage/pallas_call | solution.py:184
  145.5 2.8 %collective-permute-start.4 = (bf16[32,2048]{1,0:T(8,128)(2,1)S(1)}, bf16[32,2048]{1,0:T(8,128)(2,1)S(1)}, u32[]{:S(2)}, u32[]{:S(2)}) collective-permute-start(bf16[32,2048]{1,0:T(8,128)(2,1)S(1)} %stage.19), channel_id=1, source_target_pairs={{0,2},{2,4},{1,3},{3,5},{16,18},{18,20},{17,19},{19,21},{32,34},{3... | collective-permute-start | bytes 393224 | tf_op jit(solution)/shard_map/ppermute | solution.py:241
  148.3 3.7 %stage.27 = bf16[32,2048]{1,0:T(8,128)(2,1)S(1)} custom-call(s32[1]{0:T(128)} %bitcast.position_ref, bf16[128,2048]{1,0:T(8,128)(2,1)S(1)} %pad_maximum_fusion.refs_0_, bf16[32,2048]{1,0:T(8,128)(2,1)S(1)} %collective-permute-done.11.refs_1_, f32[2,2048]{1,0:T(2,128)S(1)} %bitcast.12, bf16[2,2048,2048]{2,1,0:T(8,128)(2,1)S(1)} %load_weights.1.refs_2_.refs_3_), custom_call_target="tpu_custom_call" | custom-call | tf_op jit(solution)/shard_map/stage/pallas_call | solution.py:184
  152.0 1.9 collective-permute-start.12
  154.7 1.9 collective-permute-done.12.refs_0_
  165.2 1.3 collective-permute-start.20
  167.2 60.2 %collective-permute-done.20.refs_3_ = bf16[32,2048]{1,0:T(8,128)(2,1)S(1)} collective-permute-done((bf16[32,2048]{1,0:T(8,128)(2,1)S(1)}, bf16[32,2048]{1,0:T(8,128)(2,1)S(1)}, u32[]{:S(2)}, u32[]{:S(2)}) %collective-permute-start.20) | collective-permute-done | bytes 131104 | tf_op jit(solution)/shard_map/ppermute | solution.py:241
  (64 shorter events, 14.3 us)
Async XLA Ops:
  6.5 117.5 %all-gather.3.cloned.1.call-start = ((), (), s32[]{:S(2)}) async-start(), calls=%async_computation.2 | async-start | bytes 17039360 | tf_op jit(solution)/shard_map/all_gather | solution.py:262
  56.2 12.4 %collective-permute-start = (bf16[16,2048]{1,0:T(8,128)(2,1)S(1)}, bf16[16,2048]{1,0:T(8,128)(2,1)S(1)}, u32[]{:S(2)}, u32[]{:S(2)}) collective-permute-start(bf16[16,2048]{1,0:T(8,128)(2,1)S(1)} %reduce_sum.12), channel_id=1, source_target_pairs={{14,0},{2,4},{6,8},{10,12},{15,1},{3,5},{7,9},{11,13},{30,16},{18,... | collective-permute-start | bytes 196616 | tf_op jit(solution)/shard_map/ppermute | solution.py:221
  68.6 7.8 %collective-permute-start.1 = (bf16[32,2048]{1,0:T(8,128)(2,1)S(1)}, bf16[32,2048]{1,0:T(8,128)(2,1)S(1)}, u32[]{:S(2)}, u32[]{:S(2)}) collective-permute-start(bf16[32,2048]{1,0:T(8,128)(2,1)S(1)} %pad_maximum_fusion.2), channel_id=1, source_target_pairs={{4,0},{12,8},{5,1},{13,9},{20,16},{28,24},{21,17},{29,25},{36,32},... | collective-permute-start | bytes 393224 | tf_op jit(solution)/shard_map/ppermute | solution.py:222
  76.4 12.2 %collective-permute-start.2 = (bf16[64,2048]{1,0:T(8,128)(2,1)S(1)}, bf16[64,2048]{1,0:T(8,128)(2,1)S(1)}, u32[]{:S(2)}, u32[]{:S(2)}) collective-permute-start(bf16[64,2048]{1,0:T(8,128)(2,1)S(1)} %pad_maximum_fusion.1), channel_id=1, source_target_pairs={{8,0},{9,1},{24,16},{25,17},{40,32},{41,33},{56,48},{57,49},{72,64... | collective-permute-start | bytes 786440 | tf_op jit(solution)/shard_map/ppermute | solution.py:223
  124.1 5.8 %copy-start = (bf16[64,64,2048]{2,1,0:T(8,128)(2,1)S(1)}, bf16[64,64,2048]{2,1,0:T(8,128)(2,1)}, u32[]{:S(2)}) copy-start(bf16[64,64,2048]{2,1,0:T(8,128)(2,1)} %all-gather.3.cloned.1.call-done) | copy-start | bytes 50331652
  135.4 6.3 %collective-permute-start.3 = (bf16[32,2048]{1,0:T(8,128)(2,1)S(1)}, bf16[32,2048]{1,0:T(8,128)(2,1)S(1)}, u32[]{:S(2)}, u32[]{:S(2)}) collective-permute-start(bf16[32,2048]{1,0:T(8,128)(2,1)S(1)} %stage.18), channel_id=1, source_target_pairs={{0,2},{1,3},{16,18},{17,19},{32,34},{33,35},{48,50},{49,51},{64,66... | collective-permute-start | bytes 393224 | tf_op jit(solution)/shard_map/ppermute | solution.py:241
  140.4 7.8 %collective-permute-start.11 = (bf16[32,2048]{1,0:T(8,128)(2,1)S(1)}, bf16[32,2048]{1,0:T(8,128)(2,1)S(1)}, u32[]{:S(2)}, u32[]{:S(2)}) collective-permute-start(bf16[32,2048]{1,0:T(8,128)(2,1)S(1)} %stage.26), channel_id=1, source_target_pairs={{0,2},{1,3},{16,18},{17,19},{32,34},{33,35},{48,50},{49,51},{64,66... | collective-permute-start | bytes 393224 | tf_op jit(solution)/shard_map/ppermute | solution.py:241
  145.5 8.4 %collective-permute-start.4 = (bf16[32,2048]{1,0:T(8,128)(2,1)S(1)}, bf16[32,2048]{1,0:T(8,128)(2,1)S(1)}, u32[]{:S(2)}, u32[]{:S(2)}) collective-permute-start(bf16[32,2048]{1,0:T(8,128)(2,1)S(1)} %stage.19), channel_id=1, source_target_pairs={{0,2},{2,4},{1,3},{3,5},{16,18},{18,20},{17,19},{19,21},{32,34},{3... | collective-permute-start | bytes 393224 | tf_op jit(solution)/shard_map/ppermute | solution.py:241
  152.0 4.5 %collective-permute-start.12 = (bf16[32,2048]{1,0:T(8,128)(2,1)S(1)}, bf16[32,2048]{1,0:T(8,128)(2,1)S(1)}, u32[]{:S(2)}, u32[]{:S(2)}) collective-permute-start(bf16[32,2048]{1,0:T(8,128)(2,1)S(1)} %stage.27), channel_id=1, source_target_pairs={{0,2},{2,4},{1,3},{3,5},{16,18},{18,20},{17,19},{19,21},{32,34},{3... | collective-permute-start | bytes 393224 | tf_op jit(solution)/shard_map/ppermute | solution.py:241
  154.0 3.2 %collective-permute-start.5 = (bf16[32,2048]{1,0:T(8,128)(2,1)S(1)}, bf16[32,2048]{1,0:T(8,128)(2,1)S(1)}, u32[]{:S(2)}, u32[]{:S(2)}) collective-permute-start(bf16[32,2048]{1,0:T(8,128)(2,1)S(1)} %stage.20), channel_id=1, source_target_pairs={{2,4},{4,6},{3,5},{5,7},{18,20},{20,22},{19,21},{21,23},{34,36},{3... | collective-permute-start | bytes 393224 | tf_op jit(solution)/shard_map/ppermute | solution.py:241
  156.5 1.4 collective-permute-start.13
  157.2 1.4 collective-permute-start.6
  157.9 1.4 collective-permute-start.14
  158.6 1.4 collective-permute-start.7
  159.3 1.4 collective-permute-start.15
  160.0 1.4 collective-permute-start.8
  160.7 1.6 collective-permute-start.16
  161.6 1.4 collective-permute-start.9
  162.3 1.4 collective-permute-start.17
  163.0 1.4 collective-permute-start.10
  163.7 1.4 collective-permute-start.18
  164.5 2.0 collective-permute-start.19
  165.2 62.3 %collective-permute-start.20 = (bf16[32,2048]{1,0:T(8,128)(2,1)S(1)}, bf16[32,2048]{1,0:T(8,128)(2,1)S(1)}, u32[]{:S(2)}, u32[]{:S(2)}) collective-permute-start(bf16[32,2048]{1,0:T(8,128)(2,1)S(1)} %stage.35.refs_5_), channel_id=1, source_target_pairs={{14,0},{15,1},{30,16},{31,17},{46,32},{47,33},{62,48},{63,49},{78,... | collective-permute-start | bytes 393224 | tf_op jit(solution)/shard_map/ppermute | solution.py:241
  166.5 60.9 %collective-permute-start.21 = (bf16[16,2048]{1,0:T(8,128)(2,1)S(1)}, bf16[16,2048]{1,0:T(8,128)(2,1)S(1)}, u32[]{:S(2)}, u32[]{:S(2)}) collective-permute-start(bf16[16,2048]{1,0:T(8,128)(2,1)S(1)} %choose.2), channel_id=1, source_target_pairs={{4,2},{8,6},{12,10},{5,3},{9,7},{13,11},{20,18},{24,22},{28,26},{2... | collective-permute-start | bytes 196616 | tf_op jit(solution)/shard_map/ppermute | solution.py:246
  (4 other events, 3.2 us)
Sparse Core Ops, SparseCore 0:
  10.7 113.3 all-gather.2

commit v3 on v2

--- a/solution.py
+++ b/solution.py
@@ -101,57 +101,93 @@
     return out.reshape(groups, CARD_DEV, width)
 
 
-def load_kernel(gathered_ref, out_ref, sem):
-    blocks, layers, rows, width = gathered_ref.shape
-    copies = [
-        pltpu.make_async_copy(
-            gathered_ref.at[b, layer], out_ref.at[layer, pl.ds(b * rows, rows)], sem.at[b, layer]
+def start_layer(out_ref, gain_ref, normed_ref, layer):
+    u = out_ref[...].astype(jnp.float32)
+    mean_sq = jnp.mean(u * u, axis=-1, keepdims=True)
+    normed = u * lax.rsqrt(mean_sq + 1e-05) * gain_ref[pl.ds(layer, 1), :]
+    normed_ref[...] = normed.astype(jnp.bfloat16)
+
+
+def add_columns(out_ref, weight_ref, normed_ref, layer, block):
+    width = out_ref.shape[1]
+    columns = pl.ds(pl.multiple_of(block * BLOCK, BLOCK), BLOCK)
+    y = jnp.dot(
+        normed_ref[...],
+        weight_ref[:, layer, :, columns].reshape(width, BLOCK),
+        preferred_element_type=jnp.float32,
+    )
+    u = out_ref[:, columns].astype(jnp.float32)
+    out_ref[:, columns] = (u + y / (1.0 + jnp.exp(-y))).astype(jnp.bfloat16)
+
+
+def run_layers(out_ref, gain_ref, weight_ref, normed_ref):
+    def layer_of(layer, carry):
+        start_layer(out_ref, gain_ref, normed_ref, layer)
+
+        def columns_of(block, carry):
+            add_columns(out_ref, weight_ref, normed_ref, layer, block)
+            return carry
+
+        return lax.fori_loop(0, out_ref.shape[1] // BLOCK, columns_of, carry)
+
+    lax.fori_loop(0, weight_ref.shape[1], layer_of, 0)
+
+
+def first_kernel(
+    position_ref, queue_ref, gain_ref, gathered_ref, out_ref, weight_ref, normed_ref, sem, *, fresh
+):
+    layers = gathered_ref.shape[1]
+    blocks = out_ref.shape[1] // BLOCK
+
+    def copy_of(layer, block):
+        columns = pl.ds(block * BLOCK, BLOCK)
+        return pltpu.make_async_copy(
+            gathered_ref.at[:, layer, :, columns],
+            weight_ref.at[:, layer, :, columns],
+            sem.at[layer, block],
         )
-        for b in range(blocks)
-        for layer in range(layers)
-    ]
-    for copy in copies:
-        copy.start()
-    for copy in copies:
-        copy.wait()
-
-
-def load_weights(gathered):
-    blocks, layers, rows, width = gathered.shape
+
+    copies = [[copy_of(layer, block) for block in range(blocks)] for layer in range(layers)]
+    for row in copies:
+        for copy in row:
+            copy.start()
+    active = position_ref[0] == 0
+
+    @pl.when(active)
+    def _():
+        out_ref[...] = queue_ref[fresh : fresh + BATCH, :]
+        for layer in range(layers):
+            start_layer(out_ref, gain_ref, normed_ref, layer)
+            for block in range(blocks):
+                copies[layer][block].wait()
+                add_columns(out_ref, weight_ref, normed_ref, layer, block)
+
+    @pl.when(jnp.logical_not(active))
+    def _():
+        for row in copies:
+            for copy in row:
+                copy.wait()
+
+
+def first_stage(position, queue, gain, gathered, fresh):
+    shape = (BATCH, gain.shape[1])
     return pl.pallas_call(
-        load_kernel,
-        out_shape=pltpu.VMEM((layers, blocks * rows, width), jnp.bfloat16),
-        in_specs=[pl.BlockSpec(memory_space=pltpu.MemorySpace.HBM)],
-        out_specs=pl.BlockSpec(memory_space=VMEM),
-        scratch_shapes=[pltpu.SemaphoreType.DMA((blocks, layers))],
-        compiler_params=pltpu.CompilerParams(vmem_limit_bytes=20 * MIB),
-        name="load_weights",
-    )(gathered)
-
-
-def run_layers(out_ref, gain_ref, weight_ref, normed_ref):
-    width = out_ref.shape[1]
-
-    def layer_of(layer, carry):
-        u = out_ref[...].astype(jnp.float32)
-        mean_sq = jnp.mean(u * u, axis=-1, keepdims=True)
-        normed = u * lax.rsqrt(mean_sq + 1e-05) * gain_ref[pl.ds(layer, 1), :]
-        normed_ref[...] = normed.astype(jnp.bfloat16)
-
-        def columns_of(block, carry):
-            columns = pl.ds(pl.multiple_of(block * BLOCK, BLOCK), BLOCK)
-            y = jnp.dot(
-                normed_ref[...],
-                weight_ref[layer, :, columns],
-                preferred_element_type=jnp.float32,
-            )
-            u = out_ref[:, columns].astype(jnp.float32)
-            out_ref[:, columns] = (u + y / (1.0 + jnp.exp(-y))).astype(jnp.bfloat16)
-            return carry
-
-        return lax.fori_loop(0, width // BLOCK, columns_of, carry)
-
-    lax.fori_loop(0, weight_ref.shape[0], layer_of, 0)
+        functools.partial(first_kernel, fresh=fresh),
+        out_shape=(
+            jax.ShapeDtypeStruct(shape, jnp.bfloat16),
+            pltpu.VMEM(gathered.shape, jnp.bfloat16),
+        ),
+        in_specs=[pl.BlockSpec(memory_space=SMEM)]
+        + [pl.BlockSpec(memory_space=VMEM)] * 2
+        + [pl.BlockSpec(memory_space=pltpu.MemorySpace.HBM)],
+        out_specs=(pl.BlockSpec(memory_space=VMEM),) * 2,
+        scratch_shapes=[
+            pltpu.VMEM(shape, jnp.bfloat16),
+            pltpu.SemaphoreType.DMA((gathered.shape[1], gain.shape[1] // BLOCK)),
+        ],
+        compiler_params=pltpu.CompilerParams(vmem_limit_bytes=24 * MIB),
+        name="first_stage",
+    )(position, queue, gain, pltpu.with_memory_space_constraint(gathered, pltpu.MemorySpace.HBM))
 
 
 def stage_kernel(position_ref, *refs, step, fresh):
@@ -223,7 +259,11 @@
     return jnp.concatenate([fours, lax.ppermute(fours, "z", [(4, 0)])])
 
 
-def tower(position, queue, gain, weight):
+def crossing(moves):
+    return [(C * a + c, C * b + C - 1 - c) for a, b in moves for c in range(C)]
+
+
+def tower(position, queue, gain, gathered):
     streams = [
         dict(fresh=(2 * CARD_DEV, 6 * CARD_DEV), home=(2, 6)),
         dict(fresh=(4 * CARD_DEV, 0), home=(4, 0)),
@@ -234,25 +274,32 @@
     for step in range(Z - 1 + TURNS):
         for s, stream in enumerate(streams):
             fresh = stream["fresh"][step] if step < TURNS else None
-            done[s] = stage(position, queue, came[s], gain, weight, step, fresh)
+            if step == 0 and s == 0:
+                done[s], weight = first_stage(position, queue, gain, gathered, fresh)
+            else:
+                done[s] = stage(position, queue, came[s], gain, weight, step, fresh)
             moves = [(z, z + 1) for z in range(Z - 1) if 0 <= step - z < TURNS]
             if step >= Z - 1:
                 moves.append((Z - 1, stream["home"][step - Z + 1]))
-            came[s] = lax.ppermute(done[s], "z", moves)
+            came[s] = lax.ppermute(done[s], ("z", "c"), crossing(moves))
             if step >= Z - 1:
                 kept[s].append(came[s])
     (two, six), (four, zero) = kept
-    lent = choose(position, [two, four, six], (((2,), 0, 0), ((4,), 1, 0), ((6,), 2, 0)))
-    lent = lax.ppermute(lent, "z", [(2, 1), (4, 3), (6, 5)])
+    lent = choose(
+        position,
+        [two, four, six, done[1]],
+        (((2,), 0, 0), ((4,), 1, 0), ((6,), 2, 0), ((Z - 1,), 3, 0)),
+    )
+    straight = [(C * a + c, C * b + c) for a, b in ((2, 1), (4, 3), (6, 5)) for c in range(C)]
+    lent = lax.ppermute(lent, ("z", "c"), straight + crossing([(Z - 1, Z - 1)]))
     cases = (
         ((2,), 0, CARD_DEV),
         ((4,), 1, CARD_DEV),
         ((6,), 2, CARD_DEV),
         ((0,), 3, CARD_DEV),
-        ((1, 3, 5), 4, 0),
-        ((7,), 5, 0),
-    )
-    return choose(position, [two, four, six, zero, lent, done[1]], cases)
+        ((1, 3, 5, 7), 4, 0),
+    )
+    return choose(position, [two, four, six, zero, lent], cases)
 
 
 def body(txn_feats, txn_seg, seg_row, send_counts, gains, tower_w):
@@ -267,7 +314,7 @@
     shares = lax.all_to_all(dense, "y", 0, 0, tiled=True)
     pooled = jnp.sum(shares.astype(jnp.float32), axis=0).astype(jnp.bfloat16)
     queue = collect(pooled)
-    weight = load_weights(gathered.reshape(X * Y, C, *tower_w.shape[1:]))
+    weight = gathered.reshape(X * Y, C, *tower_w.shape[1:])
     position = lax.axis_index("z").reshape(1)
     return tower(position, queue, gain, weight)
 

time: 235 us -> 236 us (level)
  the two profiles are of different devices: /device:TPU:24 before, /device:TPU:1 now
where the time goes in v3:
time: 236 us; the launch traced here: 235 us
  waiting for transfers between devices  118 us (50%)
  blocking collectives  57.1 us (24%)
  starting transfers between devices  22.5 us (10%)
  Pallas kernels  20 us (8%)
  between operations  13.9 us (6%)
  local copies, waits for them, and re-layouts  3.24 us (1%)
    ppermute x18, waiting for transfers between devices, tower(): came[s] = lax.ppermute(done[s], ('z', 'c'), crossing(moves))  64.5 us
    all_gather x1, waiting for transfers between devices, body(): gathered = lax.all_gather(tower_w[0], ('x', 'y', 'c'), axis=0, tiled=False)  42.1 us
    all_to_all x1, blocking collectives, body(): shares = lax.all_to_all(dense, 'y', 0, 0, tiled=True)  31.6 us
    ppermute x18, starting transfers between devices, tower(): came[s] = lax.ppermute(done[s], ('z', 'c'), crossing(moves))  18 us
    all_to_all x1, blocking collectives, body(): lax.all_to_all(buffer.reshape(X, Y * cap, width + LANES), 'x', 0, 0, tile...  15.6 us
    pallas_call x17, Pallas kernels, stage(): pl.pallas_call(functools.partial(stage_kernel, step=step, fresh=fresh), o...  11.5 us
    all_gather x1, blocking collectives, body(): gain = lax.all_gather(gains[0], 'c', axis=0, tiled=False)  9.85 us
    pallas_call x1, Pallas kernels, first_stage(): pl.pallas_call(functools.partial(first_kernel, fresh=fresh), out_shape=(j...  6.82 us
  transfers between devices with their start and end apart: 23, of which 5 were waited for; matrix products, arithmetic and copies ran while one was open for 0% of the time, Pallas kernels for 5%

profile of v3, /device:TPU:1, one launch (start us, length us, event | category | flops | bytes accessed | tf_op | source)
XLA Modules:
  0.0 235.2 jit_solution(302494005310178899)
XLA Ops:
  6.5 0.7 all-gather.3.cloned.1.call-update
  7.3 1.2 copy-done
  8.5 0.7 copy-done.1
  9.2 0.7 copy-done.2
  11.1 15.6 %all_to_all.10.got_ref = bf16[4,64,2176]{2,1,0:T(8,128)(2,1)S(1)} all-to-all(bf16[4,64,2176]{2,1,0:T(8,128)(2,1)S(1)} %bitcast.26), channel_id=1, replica_groups=mesh['x'=4,'y'=8,'z'=8,'c'=2] {'x'}, dimensions={0} | all-to-all | bytes 2228224 | tf_op jit(solution)/shard_map/all_to_all | solution.py:312
  27.1 31.6 %all_to_all.11 = bf16[8,16,2048]{2,1,0:T(8,128)(2,1)S(1)} all-to-all(bf16[8,16,2048]{2,1,0:T(8,128)(2,1)S(1)} %bitcast.27), channel_id=1, replica_groups=mesh['x'=4,'y'=8,'z'=8,'c'=2] {'y'}, dimensions={0} | all-to-all | bytes 1048576 | tf_op jit(solution)/shard_map/all_to_all | solution.py:314
  58.8 1.3 collective-permute-start
  60.1 5.4 %collective-permute-done = bf16[16,2048]{1,0:T(8,128)(2,1)S(1)} collective-permute-done((bf16[16,2048]{1,0:T(8,128)(2,1)S(1)}, bf16[16,2048]{1,0:T(8,128)(2,1)S(1)}, u32[]{:S(2)}, u32[]{:S(2)}) %collective-permute-start) | collective-permute-done | bytes 65568 | tf_op jit(solution)/shard_map/ppermute | solution.py:257
  65.5 1.3 collective-permute-start.1
  66.8 5.6 %collective-permute-done.1 = bf16[32,2048]{1,0:T(8,128)(2,1)S(1)} collective-permute-done((bf16[32,2048]{1,0:T(8,128)(2,1)S(1)}, bf16[32,2048]{1,0:T(8,128)(2,1)S(1)}, u32[]{:S(2)}, u32[]{:S(2)}) %collective-permute-start.1) | collective-permute-done | bytes 131104 | tf_op jit(solution)/shard_map/ppermute | solution.py:258
  72.4 1.3 collective-permute-start.2
  73.7 9.9 %all-gather = f32[2,1,2048]{2,1,0:T(1,128)S(1)} all-gather(f32[1,1,2048]{2,1,0:T(1,128)} %bitcast.29), channel_id=1, replica_groups=mesh['x'=4,'y'=8,'z'=8,'c'=2] {'c'}, dimensions={0}, use_global_device_ids=true | all-gather | bytes 24576 | tf_op jit(solution)/shard_map/all_gather | solution.py:310
  83.6 42.1 %all-gather.3.cloned.1.call-done = bf16[64,64,2048]{2,1,0:T(8,128)(2,1)} async-done(((bf16[1,64,2048]{2,1,0:T(8,128)(2,1)}), bf16[64,64,2048]{2,1,0:T(8,128)(2,1)}) %all-gather.3.cloned.1.call-update) | async-done | bytes 16777232 | tf_op jit(solution)/shard_map/all_gather | solution.py:309
  125.8 6.8 %first_stage.1 = (bf16[32,2048]{1,0:T(8,128)(2,1)S(1)}, bf16[32,2,64,2048]{3,2,1,0:T(8,128)(2,1)S(1)}) custom-call(s32[1]{0:T(128)} %bitcast.position_ref, bf16[128,2048]{1,0:T(8,128)(2,1)S(1)} %pad_maximum_fusion.queue_ref.refs_0_, f32[2,2048]{1,0:T(2,128)S(1)} %bitcast.8, bf16[32,2,64,2048]{3,2,1,0:T(8,128)(2,1)} %bitcast.28), custom_call_target="tpu_custom_call" | custom-call | tf_op jit(solution)/shard_map/first_stage/pallas_call | solution.py:174
  132.6 2.6 %collective-permute-start.3 = (bf16[32,2048]{1,0:T(8,128)(2,1)S(1)}, bf16[32,2048]{1,0:T(8,128)(2,1)S(1)}, u32[]{:S(2)}, u32[]{:S(2)}) collective-permute-start(bf16[32,2048]{1,0:T(8,128)(2,1)S(1)} %get-tuple-element.7), channel_id=1, source_target_pairs={{0,3},{1,2},{16,19},{17,18},{32,35},{33,34},{48,51},{49,50},{64,67... | collective-permute-start | bytes 393224 | tf_op jit(solution)/shard_map/ppermute | solution.py:284
  135.2 3.7 %stage.24 = bf16[32,2048]{1,0:T(8,128)(2,1)S(1)} custom-call(s32[1]{0:T(128)} %bitcast.position_ref, bf16[128,2048]{1,0:T(8,128)(2,1)S(1)} %pad_maximum_fusion.queue_ref.refs_0_, f32[2,2048]{1,0:T(2,128)S(1)} %bitcast.9, bf16[32,2,64,2048]{3,2,1,0:T(8,128)(2,1)S(1)} %get-tuple-element.8.refs_3_.refs_2_), custom_call_target="tpu_custom_call" | custom-call | tf_op jit(solution)/shard_map/stage/pallas_call | solution.py:220
  138.9 1.3 collective-permute-start.11
  140.2 3.7 %stage.17 = bf16[32,2048]{1,0:T(8,128)(2,1)S(1)} custom-call(s32[1]{0:T(128)} %bitcast.position_ref, bf16[128,2048]{1,0:T(8,128)(2,1)S(1)} %pad_maximum_fusion.queue_ref.refs_0_, bf16[32,2048]{1,0:T(8,128)(2,1)S(1)} %collective-permute-done.3.refs_1_, f32[2,2048]{1,0:T(2,128)S(1)} %bitcast.10, bf16[32,2,64,2048]{3,2,1,0:T(8,128)(2,1)S(1)} %get-tuple-element.8.refs_3_.refs_2_), custom_call_target="tpu_custom_call" | custom-call | tf_op jit(solution)/shard_map/stage/pallas_call | solution.py:220
  144.0 2.2 collective-permute-start.4
  146.2 3.7 %stage.25 = bf16[32,2048]{1,0:T(8,128)(2,1)S(1)} custom-call(s32[1]{0:T(128)} %bitcast.position_ref, bf16[128,2048]{1,0:T(8,128)(2,1)S(1)} %pad_maximum_fusion.queue_ref.refs_0_, bf16[32,2048]{1,0:T(8,128)(2,1)S(1)} %collective-permute-done.11.refs_1_, f32[2,2048]{1,0:T(2,128)S(1)} %bitcast.11, bf16[32,2,64,2048]{3,2,1,0:T(8,128)(2,1)S(1)} %get-tuple-element.8.refs_3_.refs_2_), custom_call_target="tpu_custom_call" | custom-call | tf_op jit(solution)/shard_map/stage/pallas_call | solution.py:220
  149.9 1.9 collective-permute-start.12
  152.5 2.2 collective-permute-done.12.refs_0_
  163.3 1.3 collective-permute-start.20
  165.4 62.3 %collective-permute-done.20.refs_3_ = bf16[32,2048]{1,0:T(8,128)(2,1)S(1)} collective-permute-done((bf16[32,2048]{1,0:T(8,128)(2,1)S(1)}, bf16[32,2048]{1,0:T(8,128)(2,1)S(1)}, u32[]{:S(2)}, u32[]{:S(2)}) %collective-permute-start.20) | collective-permute-done | bytes 131104 | tf_op jit(solution)/shard_map/ppermute | solution.py:284
  (61 shorter events, 12.2 us)
Async XLA Ops:
  6.5 119.2 %all-gather.3.cloned.1.call-start = ((), (), s32[]{:S(2)}) async-start(), calls=%async_computation.2 | async-start | bytes 17039360 | tf_op jit(solution)/shard_map/all_gather | solution.py:309
  7.3 1.2 copy-start
  58.8 6.7 %collective-permute-start = (bf16[16,2048]{1,0:T(8,128)(2,1)S(1)}, bf16[16,2048]{1,0:T(8,128)(2,1)S(1)}, u32[]{:S(2)}, u32[]{:S(2)}) collective-permute-start(bf16[16,2048]{1,0:T(8,128)(2,1)S(1)} %reduce_sum.12), channel_id=1, source_target_pairs={{14,0},{2,4},{6,8},{10,12},{15,1},{3,5},{7,9},{11,13},{30,16},{18,... | collective-permute-start | bytes 196616 | tf_op jit(solution)/shard_map/ppermute | solution.py:257
  65.5 6.9 %collective-permute-start.1 = (bf16[32,2048]{1,0:T(8,128)(2,1)S(1)}, bf16[32,2048]{1,0:T(8,128)(2,1)S(1)}, u32[]{:S(2)}, u32[]{:S(2)}) collective-permute-start(bf16[32,2048]{1,0:T(8,128)(2,1)S(1)} %pad_maximum_fusion.2), channel_id=1, source_target_pairs={{4,0},{12,8},{5,1},{13,9},{20,16},{28,24},{21,17},{29,25},{36,32},... | collective-permute-start | bytes 393224 | tf_op jit(solution)/shard_map/ppermute | solution.py:258
  72.4 11.2 %collective-permute-start.2 = (bf16[64,2048]{1,0:T(8,128)(2,1)S(1)}, bf16[64,2048]{1,0:T(8,128)(2,1)S(1)}, u32[]{:S(2)}, u32[]{:S(2)}) collective-permute-start(bf16[64,2048]{1,0:T(8,128)(2,1)S(1)} %pad_maximum_fusion.1), channel_id=1, source_target_pairs={{8,0},{9,1},{24,16},{25,17},{40,32},{41,33},{56,48},{57,49},{72,64... | collective-permute-start | bytes 786440 | tf_op jit(solution)/shard_map/ppermute | solution.py:259
  132.6 7.6 %collective-permute-start.3 = (bf16[32,2048]{1,0:T(8,128)(2,1)S(1)}, bf16[32,2048]{1,0:T(8,128)(2,1)S(1)}, u32[]{:S(2)}, u32[]{:S(2)}) collective-permute-start(bf16[32,2048]{1,0:T(8,128)(2,1)S(1)} %get-tuple-element.7), channel_id=1, source_target_pairs={{0,3},{1,2},{16,19},{17,18},{32,35},{33,34},{48,51},{49,50},{64,67... | collective-permute-start | bytes 393224 | tf_op jit(solution)/shard_map/ppermute | solution.py:284
  138.9 7.3 %collective-permute-start.11 = (bf16[32,2048]{1,0:T(8,128)(2,1)S(1)}, bf16[32,2048]{1,0:T(8,128)(2,1)S(1)}, u32[]{:S(2)}, u32[]{:S(2)}) collective-permute-start(bf16[32,2048]{1,0:T(8,128)(2,1)S(1)} %stage.24), channel_id=1, source_target_pairs={{0,3},{1,2},{16,19},{17,18},{32,35},{33,34},{48,51},{49,50},{64,67... | collective-permute-start | bytes 393224 | tf_op jit(solution)/shard_map/ppermute | solution.py:284
  144.0 7.9 %collective-permute-start.4 = (bf16[32,2048]{1,0:T(8,128)(2,1)S(1)}, bf16[32,2048]{1,0:T(8,128)(2,1)S(1)}, u32[]{:S(2)}, u32[]{:S(2)}) collective-permute-start(bf16[32,2048]{1,0:T(8,128)(2,1)S(1)} %stage.17), channel_id=1, source_target_pairs={{0,3},{1,2},{2,5},{3,4},{16,19},{17,18},{18,21},{19,20},{32,35},{3... | collective-permute-start | bytes 393224 | tf_op jit(solution)/shard_map/ppermute | solution.py:284
  149.9 4.8 %collective-permute-start.12 = (bf16[32,2048]{1,0:T(8,128)(2,1)S(1)}, bf16[32,2048]{1,0:T(8,128)(2,1)S(1)}, u32[]{:S(2)}, u32[]{:S(2)}) collective-permute-start(bf16[32,2048]{1,0:T(8,128)(2,1)S(1)} %stage.25), channel_id=1, source_target_pairs={{0,3},{1,2},{2,5},{3,4},{16,19},{17,18},{18,21},{19,20},{32,35},{3... | collective-permute-start | bytes 393224 | tf_op jit(solution)/shard_map/ppermute | solution.py:284
  151.9 3.5 %collective-permute-start.5 = (bf16[32,2048]{1,0:T(8,128)(2,1)S(1)}, bf16[32,2048]{1,0:T(8,128)(2,1)S(1)}, u32[]{:S(2)}, u32[]{:S(2)}) collective-permute-start(bf16[32,2048]{1,0:T(8,128)(2,1)S(1)} %stage.18), channel_id=1, source_target_pairs={{2,5},{3,4},{4,7},{5,6},{18,21},{19,20},{20,23},{21,22},{34,37},{3... | collective-permute-start | bytes 393224 | tf_op jit(solution)/shard_map/ppermute | solution.py:284
  154.7 1.4 collective-permute-start.13
  155.4 1.4 collective-permute-start.6
  156.1 1.4 collective-permute-start.14
  156.8 1.4 collective-permute-start.7
  157.5 1.4 collective-permute-start.15
  158.2 1.4 collective-permute-start.8
  158.9 1.6 collective-permute-start.16
  159.8 1.4 collective-permute-start.9
  160.5 1.4 collective-permute-start.17
  161.2 1.4 collective-permute-start.10
  161.9 1.4 collective-permute-start.18
  162.6 2.0 collective-permute-start.19
  163.3 64.4 %collective-permute-start.20 = (bf16[32,2048]{1,0:T(8,128)(2,1)S(1)}, bf16[32,2048]{1,0:T(8,128)(2,1)S(1)}, u32[]{:S(2)}, u32[]{:S(2)}) collective-permute-start(bf16[32,2048]{1,0:T(8,128)(2,1)S(1)} %stage.33.refs_3_), channel_id=1, source_target_pairs={{14,1},{15,0},{30,17},{31,16},{46,33},{47,32},{62,49},{63,48},{78,... | collective-permute-start | bytes 393224 | tf_op jit(solution)/shard_map/ppermute | solution.py:284
  164.7 63.0 %collective-permute-start.21 = (bf16[16,2048]{1,0:T(8,128)(2,1)S(1)}, bf16[16,2048]{1,0:T(8,128)(2,1)S(1)}, u32[]{:S(2)}, u32[]{:S(2)}) collective-permute-start(bf16[16,2048]{1,0:T(8,128)(2,1)S(1)} %choose.2), channel_id=1, source_target_pairs={{4,2},{5,3},{8,6},{9,7},{12,10},{13,11},{14,15},{15,14},{20,18},{2... | collective-permute-start | bytes 196616 | tf_op jit(solution)/shard_map/ppermute | solution.py:294
  (3 other events, 2.0 us)
Sparse Core Ops, SparseCore 0:
  10.7 115.0 all-gather.2

commit v4 on v3

--- a/solution.py
+++ b/solution.py
@@ -259,10 +259,6 @@
     return jnp.concatenate([fours, lax.ppermute(fours, "z", [(4, 0)])])
 
 
-def crossing(moves):
-    return [(C * a + c, C * b + C - 1 - c) for a, b in moves for c in range(C)]
-
-
 def tower(position, queue, gain, gathered):
     streams = [
         dict(fresh=(2 * CARD_DEV, 6 * CARD_DEV), home=(2, 6)),
@@ -281,25 +277,21 @@
             moves = [(z, z + 1) for z in range(Z - 1) if 0 <= step - z < TURNS]
             if step >= Z - 1:
                 moves.append((Z - 1, stream["home"][step - Z + 1]))
-            came[s] = lax.ppermute(done[s], ("z", "c"), crossing(moves))
+            came[s] = lax.ppermute(done[s], "z", moves)
             if step >= Z - 1:
                 kept[s].append(came[s])
     (two, six), (four, zero) = kept
-    lent = choose(
-        position,
-        [two, four, six, done[1]],
-        (((2,), 0, 0), ((4,), 1, 0), ((6,), 2, 0), ((Z - 1,), 3, 0)),
-    )
-    straight = [(C * a + c, C * b + c) for a, b in ((2, 1), (4, 3), (6, 5)) for c in range(C)]
-    lent = lax.ppermute(lent, ("z", "c"), straight + crossing([(Z - 1, Z - 1)]))
+    lent = choose(position, [two, four, six], (((2,), 0, 0), ((4,), 1, 0), ((6,), 2, 0)))
+    lent = lax.ppermute(lent, "z", [(2, 1), (4, 3), (6, 5)])
     cases = (
         ((2,), 0, CARD_DEV),
         ((4,), 1, CARD_DEV),
         ((6,), 2, CARD_DEV),
         ((0,), 3, CARD_DEV),
-        ((1, 3, 5, 7), 4, 0),
-    )
-    return choose(position, [two, four, six, zero, lent], cases)
+        ((1, 3, 5), 4, 0),
+        ((7,), 5, 0),
+    )
+    return choose(position, [two, four, six, zero, lent, done[1]], cases)
 
 
 def body(txn_feats, txn_seg, seg_row, send_counts, gains, tower_w):

time: 236 us -> 232 us (0.983)
  the two profiles are of different devices: /device:TPU:1 before, /device:TPU:24 now
where the time goes in v4:
time: 232 us; the launch traced here: 231 us
  waiting for transfers between devices  124 us (53%)
  blocking collectives  46.6 us (20%)
  starting transfers between devices  22.9 us (10%)
  Pallas kernels  20 us (9%)
  between operations  13.9 us (6%)
  local copies, waits for them, and re-layouts  3.24 us (1%)
    ppermute x18, waiting for transfers between devices, tower(): came[s] = lax.ppermute(done[s], 'z', moves)  61.8 us
    all_gather x1, waiting for transfers between devices, body(): gathered = lax.all_gather(tower_w[0], ('x', 'y', 'c'), axis=0, tiled=False)  35.4 us
    all_to_all x1, blocking collectives, body(): shares = lax.all_to_all(dense, 'y', 0, 0, tiled=True)  24.7 us
    all_to_all x1, blocking collectives, body(): lax.all_to_all(buffer.reshape(X, Y * cap, width + LANES), 'x', 0, 0, tile...  19.9 us
    ppermute x18, starting transfers between devices, tower(): came[s] = lax.ppermute(done[s], 'z', moves)  18.4 us
    pallas_call x17, Pallas kernels, stage(): pl.pallas_call(functools.partial(stage_kernel, step=step, fresh=fresh), o...  11.5 us
    ppermute x1, waiting for transfers between devices, collect(): lax.ppermute(pooled, 'z', [(7, 0), (1, 2), (3, 4), (5, 6)])  11.1 us
    ppermute x1, waiting for transfers between devices, collect(): return jnp.concatenate([fours, lax.ppermute(fours, 'z', [(4, 0)])])  8.82 us
  transfers between devices with their start and end apart: 23, of which 6 were waited for; matrix products, arithmetic and copies ran while one was open for 0% of the time, Pallas kernels for 5%

profile of v4, /device:TPU:24, one launch (start us, length us, event | category | flops | bytes accessed | tf_op | source)
XLA Modules:
  0.0 231.2 jit_solution(883189446047784220)
XLA Ops:
  6.5 0.7 all-gather.3.cloned.1.call-update
  7.3 1.2 copy-done
  8.5 0.7 copy-done.1
  11.1 19.9 %all_to_all.10.got_ref = bf16[4,64,2176]{2,1,0:T(8,128)(2,1)S(1)} all-to-all(bf16[4,64,2176]{2,1,0:T(8,128)(2,1)S(1)} %bitcast.26), channel_id=1, replica_groups=mesh['x'=4,'y'=8,'z'=8,'c'=2] {'x'}, dimensions={0} | all-to-all | bytes 2228224 | tf_op jit(solution)/shard_map/all_to_all | solution.py:304
  31.4 24.7 %all_to_all.11 = bf16[8,16,2048]{2,1,0:T(8,128)(2,1)S(1)} all-to-all(bf16[8,16,2048]{2,1,0:T(8,128)(2,1)S(1)} %bitcast.27), channel_id=1, replica_groups=mesh['x'=4,'y'=8,'z'=8,'c'=2] {'y'}, dimensions={0} | all-to-all | bytes 1048576 | tf_op jit(solution)/shard_map/all_to_all | solution.py:306
  56.2 1.3 collective-permute-start
  57.5 11.1 %collective-permute-done = bf16[16,2048]{1,0:T(8,128)(2,1)S(1)} collective-permute-done((bf16[16,2048]{1,0:T(8,128)(2,1)S(1)}, bf16[16,2048]{1,0:T(8,128)(2,1)S(1)}, u32[]{:S(2)}, u32[]{:S(2)}) %collective-permute-start) | collective-permute-done | bytes 65568 | tf_op jit(solution)/shard_map/ppermute | solution.py:257
  68.6 1.3 collective-permute-start.1
  69.9 6.5 %collective-permute-done.1 = bf16[32,2048]{1,0:T(8,128)(2,1)S(1)} collective-permute-done((bf16[32,2048]{1,0:T(8,128)(2,1)S(1)}, bf16[32,2048]{1,0:T(8,128)(2,1)S(1)}, u32[]{:S(2)}, u32[]{:S(2)}) %collective-permute-start.1) | collective-permute-done | bytes 131104 | tf_op jit(solution)/shard_map/ppermute | solution.py:258
  76.4 1.3 collective-permute-start.2
  77.7 2.0 all-gather
  79.8 8.8 %collective-permute-done.2 = bf16[64,2048]{1,0:T(8,128)(2,1)S(1)} collective-permute-done((bf16[64,2048]{1,0:T(8,128)(2,1)S(1)}, bf16[64,2048]{1,0:T(8,128)(2,1)S(1)}, u32[]{:S(2)}, u32[]{:S(2)}) %collective-permute-start.2) | collective-permute-done | bytes 262176 | tf_op jit(solution)/shard_map/ppermute | solution.py:259
  88.6 35.4 %all-gather.3.cloned.1.call-done = bf16[64,64,2048]{2,1,0:T(8,128)(2,1)} async-done(((bf16[1,64,2048]{2,1,0:T(8,128)(2,1)}), bf16[64,64,2048]{2,1,0:T(8,128)(2,1)}) %all-gather.3.cloned.1.call-update) | async-done | bytes 16777232 | tf_op jit(solution)/shard_map/all_gather | solution.py:301
  124.1 6.8 %first_stage.1 = (bf16[32,2048]{1,0:T(8,128)(2,1)S(1)}, bf16[32,2,64,2048]{3,2,1,0:T(8,128)(2,1)S(1)}) custom-call(s32[1]{0:T(128)} %bitcast.position_ref, bf16[128,2048]{1,0:T(8,128)(2,1)S(1)} %pad_maximum_fusion.queue_ref.refs_0_, f32[2,2048]{1,0:T(2,128)S(1)} %bitcast.8, bf16[32,2,64,2048]{3,2,1,0:T(8,128)(2,1)} %bitcast.28), custom_call_target="tpu_custom_call" | custom-call | tf_op jit(solution)/shard_map/first_stage/pallas_call | solution.py:174
  130.9 2.7 %collective-permute-start.3 = (bf16[32,2048]{1,0:T(8,128)(2,1)S(1)}, bf16[32,2048]{1,0:T(8,128)(2,1)S(1)}, u32[]{:S(2)}, u32[]{:S(2)}) collective-permute-start(bf16[32,2048]{1,0:T(8,128)(2,1)S(1)} %get-tuple-element.7), channel_id=1, source_target_pairs={{0,2},{1,3},{16,18},{17,19},{32,34},{33,35},{48,50},{49,51},{64,66... | collective-permute-start | bytes 393224 | tf_op jit(solution)/shard_map/ppermute | solution.py:280
  133.6 3.7 %stage.24 = bf16[32,2048]{1,0:T(8,128)(2,1)S(1)} custom-call(s32[1]{0:T(128)} %bitcast.position_ref, bf16[128,2048]{1,0:T(8,128)(2,1)S(1)} %pad_maximum_fusion.queue_ref.refs_0_, f32[2,2048]{1,0:T(2,128)S(1)} %bitcast.9, bf16[32,2,64,2048]{3,2,1,0:T(8,128)(2,1)S(1)} %get-tuple-element.8.refs_3_.refs_2_), custom_call_target="tpu_custom_call" | custom-call | tf_op jit(solution)/shard_map/stage/pallas_call | solution.py:220
  137.3 1.3 collective-permute-start.11
  138.6 3.7 %stage.17 = bf16[32,2048]{1,0:T(8,128)(2,1)S(1)} custom-call(s32[1]{0:T(128)} %bitcast.position_ref, bf16[128,2048]{1,0:T(8,128)(2,1)S(1)} %pad_maximum_fusion.queue_ref.refs_0_, bf16[32,2048]{1,0:T(8,128)(2,1)S(1)} %collective-permute-done.3.refs_1_, f32[2,2048]{1,0:T(2,128)S(1)} %bitcast.10, bf16[32,2,64,2048]{3,2,1,0:T(8,128)(2,1)S(1)} %get-tuple-element.8.refs_3_.refs_2_), custom_call_target="tpu_custom_call" | custom-call | tf_op jit(solution)/shard_map/stage/pallas_call | solution.py:220
  142.4 2.5 %collective-permute-start.4 = (bf16[32,2048]{1,0:T(8,128)(2,1)S(1)}, bf16[32,2048]{1,0:T(8,128)(2,1)S(1)}, u32[]{:S(2)}, u32[]{:S(2)}) collective-permute-start(bf16[32,2048]{1,0:T(8,128)(2,1)S(1)} %stage.17), channel_id=1, source_target_pairs={{0,2},{2,4},{1,3},{3,5},{16,18},{18,20},{17,19},{19,21},{32,34},{3... | collective-permute-start | bytes 393224 | tf_op jit(solution)/shard_map/ppermute | solution.py:280
  144.9 3.7 %stage.25 = bf16[32,2048]{1,0:T(8,128)(2,1)S(1)} custom-call(s32[1]{0:T(128)} %bitcast.position_ref, bf16[128,2048]{1,0:T(8,128)(2,1)S(1)} %pad_maximum_fusion.queue_ref.refs_0_, bf16[32,2048]{1,0:T(8,128)(2,1)S(1)} %collective-permute-done.11.refs_1_, f32[2,2048]{1,0:T(2,128)S(1)} %bitcast.11, bf16[32,2,64,2048]{3,2,1,0:T(8,128)(2,1)S(1)} %get-tuple-element.8.refs_3_.refs_2_), custom_call_target="tpu_custom_call" | custom-call | tf_op jit(solution)/shard_map/stage/pallas_call | solution.py:220
  148.6 1.9 collective-permute-start.12
  151.2 1.8 collective-permute-done.12.refs_0_
  161.7 1.3 collective-permute-start.20
  163.7 60.0 %collective-permute-done.20.refs_3_ = bf16[32,2048]{1,0:T(8,128)(2,1)S(1)} collective-permute-done((bf16[32,2048]{1,0:T(8,128)(2,1)S(1)}, bf16[32,2048]{1,0:T(8,128)(2,1)S(1)}, u32[]{:S(2)}, u32[]{:S(2)}) %collective-permute-start.20) | collective-permute-done | bytes 131104 | tf_op jit(solution)/shard_map/ppermute | solution.py:280
  (61 shorter events, 12.9 us)
Async XLA Ops:
  6.5 117.5 %all-gather.3.cloned.1.call-start = ((), (), s32[]{:S(2)}) async-start(), calls=%async_computation.2 | async-start | bytes 17039360 | tf_op jit(solution)/shard_map/all_gather | solution.py:301
  7.3 1.2 copy-start
  56.2 12.4 %collective-permute-start = (bf16[16,2048]{1,0:T(8,128)(2,1)S(1)}, bf16[16,2048]{1,0:T(8,128)(2,1)S(1)}, u32[]{:S(2)}, u32[]{:S(2)}) collective-permute-start(bf16[16,2048]{1,0:T(8,128)(2,1)S(1)} %reduce_sum.12), channel_id=1, source_target_pairs={{14,0},{2,4},{6,8},{10,12},{15,1},{3,5},{7,9},{11,13},{30,16},{18,... | collective-permute-start | bytes 196616 | tf_op jit(solution)/shard_map/ppermute | solution.py:257
  68.6 7.8 %collective-permute-start.1 = (bf16[32,2048]{1,0:T(8,128)(2,1)S(1)}, bf16[32,2048]{1,0:T(8,128)(2,1)S(1)}, u32[]{:S(2)}, u32[]{:S(2)}) collective-permute-start(bf16[32,2048]{1,0:T(8,128)(2,1)S(1)} %pad_maximum_fusion.2), channel_id=1, source_target_pairs={{4,0},{12,8},{5,1},{13,9},{20,16},{28,24},{21,17},{29,25},{36,32},... | collective-permute-start | bytes 393224 | tf_op jit(solution)/shard_map/ppermute | solution.py:258
  76.4 12.2 %collective-permute-start.2 = (bf16[64,2048]{1,0:T(8,128)(2,1)S(1)}, bf16[64,2048]{1,0:T(8,128)(2,1)S(1)}, u32[]{:S(2)}, u32[]{:S(2)}) collective-permute-start(bf16[64,2048]{1,0:T(8,128)(2,1)S(1)} %pad_maximum_fusion.1), channel_id=1, source_target_pairs={{8,0},{9,1},{24,16},{25,17},{40,32},{41,33},{56,48},{57,49},{72,64... | collective-permute-start | bytes 786440 | tf_op jit(solution)/shard_map/ppermute | solution.py:259
  130.9 7.7 %collective-permute-start.3 = (bf16[32,2048]{1,0:T(8,128)(2,1)S(1)}, bf16[32,2048]{1,0:T(8,128)(2,1)S(1)}, u32[]{:S(2)}, u32[]{:S(2)}) collective-permute-start(bf16[32,2048]{1,0:T(8,128)(2,1)S(1)} %get-tuple-element.7), channel_id=1, source_target_pairs={{0,2},{1,3},{16,18},{17,19},{32,34},{33,35},{48,50},{49,51},{64,66... | collective-permute-start | bytes 393224 | tf_op jit(solution)/shard_map/ppermute | solution.py:280
  137.3 7.5 %collective-permute-start.11 = (bf16[32,2048]{1,0:T(8,128)(2,1)S(1)}, bf16[32,2048]{1,0:T(8,128)(2,1)S(1)}, u32[]{:S(2)}, u32[]{:S(2)}) collective-permute-start(bf16[32,2048]{1,0:T(8,128)(2,1)S(1)} %stage.24), channel_id=1, source_target_pairs={{0,2},{1,3},{16,18},{17,19},{32,34},{33,35},{48,50},{49,51},{64,66... | collective-permute-start | bytes 393224 | tf_op jit(solution)/shard_map/ppermute | solution.py:280
  142.4 8.2 %collective-permute-start.4 = (bf16[32,2048]{1,0:T(8,128)(2,1)S(1)}, bf16[32,2048]{1,0:T(8,128)(2,1)S(1)}, u32[]{:S(2)}, u32[]{:S(2)}) collective-permute-start(bf16[32,2048]{1,0:T(8,128)(2,1)S(1)} %stage.17), channel_id=1, source_target_pairs={{0,2},{2,4},{1,3},{3,5},{16,18},{18,20},{17,19},{19,21},{32,34},{3... | collective-permute-start | bytes 393224 | tf_op jit(solution)/shard_map/ppermute | solution.py:280
  148.6 4.4 %collective-permute-start.12 = (bf16[32,2048]{1,0:T(8,128)(2,1)S(1)}, bf16[32,2048]{1,0:T(8,128)(2,1)S(1)}, u32[]{:S(2)}, u32[]{:S(2)}) collective-permute-start(bf16[32,2048]{1,0:T(8,128)(2,1)S(1)} %stage.25), channel_id=1, source_target_pairs={{0,2},{2,4},{1,3},{3,5},{16,18},{18,20},{17,19},{19,21},{32,34},{3... | collective-permute-start | bytes 393224 | tf_op jit(solution)/shard_map/ppermute | solution.py:280
  150.6 3.1 %collective-permute-start.5 = (bf16[32,2048]{1,0:T(8,128)(2,1)S(1)}, bf16[32,2048]{1,0:T(8,128)(2,1)S(1)}, u32[]{:S(2)}, u32[]{:S(2)}) collective-permute-start(bf16[32,2048]{1,0:T(8,128)(2,1)S(1)} %stage.18), channel_id=1, source_target_pairs={{2,4},{4,6},{3,5},{5,7},{18,20},{20,22},{19,21},{21,23},{34,36},{3... | collective-permute-start | bytes 393224 | tf_op jit(solution)/shard_map/ppermute | solution.py:280
  153.0 1.4 collective-permute-start.13
  153.7 1.4 collective-permute-start.6
  154.4 1.4 collective-permute-start.14
  155.1 1.4 collective-permute-start.7
  155.9 1.4 collective-permute-start.15
  156.6 1.4 collective-permute-start.8
  157.3 1.6 collective-permute-start.16
  158.2 1.4 collective-permute-start.9
  158.9 1.4 collective-permute-start.17
  159.6 1.4 collective-permute-start.10
  160.3 1.4 collective-permute-start.18
  161.0 2.0 collective-permute-start.19
  161.7 62.0 %collective-permute-start.20 = (bf16[32,2048]{1,0:T(8,128)(2,1)S(1)}, bf16[32,2048]{1,0:T(8,128)(2,1)S(1)}, u32[]{:S(2)}, u32[]{:S(2)}) collective-permute-start(bf16[32,2048]{1,0:T(8,128)(2,1)S(1)} %stage.33.refs_5_), channel_id=1, source_target_pairs={{14,0},{15,1},{30,16},{31,17},{46,32},{47,33},{62,48},{63,49},{78,... | collective-permute-start | bytes 393224 | tf_op jit(solution)/shard_map/ppermute | solution.py:280
  163.0 60.6 %collective-permute-start.21 = (bf16[16,2048]{1,0:T(8,128)(2,1)S(1)}, bf16[16,2048]{1,0:T(8,128)(2,1)S(1)}, u32[]{:S(2)}, u32[]{:S(2)}) collective-permute-start(bf16[16,2048]{1,0:T(8,128)(2,1)S(1)} %choose.2), channel_id=1, source_target_pairs={{4,2},{8,6},{12,10},{5,3},{9,7},{13,11},{20,18},{24,22},{28,26},{2... | collective-permute-start | bytes 196616 | tf_op jit(solution)/shard_map/ppermute | solution.py:285
  (3 other events, 2.0 us)
Sparse Core Ops, SparseCore 0:
  10.7 113.3 all-gather.2

commit v5 on v4

--- a/solution.py
+++ b/solution.py
@@ -214,8 +214,8 @@
         run_layers(out_ref, gain_ref, weight_ref, normed_ref)
 
 
-def stage(position, queue, came, gain, weight, step, fresh):
-    sources = [a for a in (queue if fresh is not None else None, came) if a is not None]
+def stage(position, queue, came, gain, weight, step, fresh, after):
+    sources = [a for a in (queue if fresh is not None else after, came) if a is not None]
     shape = (BATCH, gain.shape[1])
     return pl.pallas_call(
         functools.partial(stage_kernel, step=step, fresh=fresh),
@@ -254,15 +254,15 @@
 
 
 def collect(pooled):
-    pairs = jnp.concatenate([lax.ppermute(pooled, "z", [(7, 0), (1, 2), (3, 4), (5, 6)]), pooled])
+    pairs = jnp.concatenate([pooled, lax.ppermute(pooled, "z", [(1, 0), (3, 2), (5, 4), (7, 6)])])
     fours = jnp.concatenate([pairs, lax.ppermute(pairs, "z", [(2, 0), (6, 4)])])
     return jnp.concatenate([fours, lax.ppermute(fours, "z", [(4, 0)])])
 
 
 def tower(position, queue, gain, gathered):
     streams = [
-        dict(fresh=(2 * CARD_DEV, 6 * CARD_DEV), home=(2, 6)),
-        dict(fresh=(4 * CARD_DEV, 0), home=(4, 0)),
+        dict(fresh=(0, 2 * BATCH), home=(0, 5)),
+        dict(fresh=(BATCH, 3 * BATCH), home=(2, 6)),
     ]
     came = [None, None]
     kept = [[], []]
@@ -273,25 +273,29 @@
             if step == 0 and s == 0:
                 done[s], weight = first_stage(position, queue, gain, gathered, fresh)
             else:
-                done[s] = stage(position, queue, came[s], gain, weight, step, fresh)
+                after = done[0] if s == 1 else None
+                done[s] = stage(position, queue, came[s], gain, weight, step, fresh, after)
             moves = [(z, z + 1) for z in range(Z - 1) if 0 <= step - z < TURNS]
             if step >= Z - 1:
                 moves.append((Z - 1, stream["home"][step - Z + 1]))
             came[s] = lax.ppermute(done[s], "z", moves)
             if step >= Z - 1:
                 kept[s].append(came[s])
-    (two, six), (four, zero) = kept
-    lent = choose(position, [two, four, six], (((2,), 0, 0), ((4,), 1, 0), ((6,), 2, 0)))
-    lent = lax.ppermute(lent, "z", [(2, 1), (4, 3), (6, 5)])
+            if step == Z and s == 0:
+                four = lax.ppermute(done[s], "z", [(Z - 1, 4)])
+    (zero, five), (two, six) = kept
+    lent = choose(position, [zero, two, four, five], (((0,), 0, CARD_DEV), ((2,), 1, CARD_DEV)))
+    lent = lax.ppermute(lent, "z", [(0, 1), (2, 3)])
     cases = (
-        ((2,), 0, CARD_DEV),
-        ((4,), 1, CARD_DEV),
-        ((6,), 2, CARD_DEV),
-        ((0,), 3, CARD_DEV),
-        ((1, 3, 5), 4, 0),
-        ((7,), 5, 0),
-    )
-    return choose(position, [two, four, six, zero, lent, done[1]], cases)
+        ((0,), 0, 0),
+        ((2,), 1, 0),
+        ((4,), 2, 0),
+        ((5,), 3, CARD_DEV),
+        ((6,), 4, 0),
+        ((1, 3), 5, 0),
+        ((7,), 6, CARD_DEV),
+    )
+    return choose(position, [zero, two, four, five, six, lent, done[1]], cases)
 
 
 def body(txn_feats, txn_seg, seg_row, send_counts, gains, tower_w):

time: 232 us -> 226 us (0.974)
  the two profiles are of different devices: /device:TPU:24 before, /device:TPU:384 now
where the time goes in v5:
time: 226 us; the launch traced here: 225 us
  waiting for transfers between devices  112 us (50%)
  blocking collectives  49.6 us (22%)
  starting transfers between devices  23.6 us (10%)
  Pallas kernels  22.6 us (10%)
  between operations  13.9 us (6%)
  local copies, waits for them, and re-layouts  3.24 us (1%)
    ppermute x18, waiting for transfers between devices, tower(): came[s] = lax.ppermute(done[s], 'z', moves)  56.2 us
    all_gather x1, waiting for transfers between devices, body(): gathered = lax.all_gather(tower_w[0], ('x', 'y', 'c'), axis=0, tiled=False)  48 us
    all_to_all x1, blocking collectives, body(): shares = lax.all_to_all(dense, 'y', 0, 0, tiled=True)  26.8 us
    all_to_all x1, blocking collectives, body(): lax.all_to_all(buffer.reshape(X, Y * cap, width + LANES), 'x', 0, 0, tile...  20.7 us
    ppermute x18, starting transfers between devices, tower(): came[s] = lax.ppermute(done[s], 'z', moves)  18.8 us
    pallas_call x17, Pallas kernels, stage(): pl.pallas_call(functools.partial(stage_kernel, step=step, fresh=fresh), o...  15 us
    pallas_call x1, Pallas kernels, first_stage(): pl.pallas_call(functools.partial(first_kernel, fresh=fresh), out_shape=(j...  5.97 us
    ppermute x1, waiting for transfers between devices, collect(): lax.ppermute(pooled, 'z', [(1, 0), (3, 2), (5, 4), (7, 6)])  4.86 us
  transfers between devices with their start and end apart: 24, of which 7 were waited for; matrix products, arithmetic and copies ran while one was open for 0% of the time, Pallas kernels for 7%

profile of v5, /device:TPU:384, one launch (start us, length us, event | category | flops | bytes accessed | tf_op | source)
XLA Modules:
  0.0 225.4 jit_solution(7747771406551433798)
XLA Ops:
  7.3 1.2 copy-done
  11.1 20.7 %all_to_all.10.got_ref = bf16[4,64,2176]{2,1,0:T(8,128)(2,1)S(1)} all-to-all(bf16[4,64,2176]{2,1,0:T(8,128)(2,1)S(1)} %bitcast.26), channel_id=1, replica_groups=mesh['x'=4,'y'=8,'z'=8,'c'=2] {'x'}, dimensions={0} | all-to-all | bytes 2228224 | tf_op jit(solution)/shard_map/all_to_all | solution.py:308
  32.2 26.8 %all_to_all.11 = bf16[8,16,2048]{2,1,0:T(8,128)(2,1)S(1)} all-to-all(bf16[8,16,2048]{2,1,0:T(8,128)(2,1)S(1)} %bitcast.27), channel_id=1, replica_groups=mesh['x'=4,'y'=8,'z'=8,'c'=2] {'y'}, dimensions={0} | all-to-all | bytes 1048576 | tf_op jit(solution)/shard_map/all_to_all | solution.py:310
  59.2 1.3 collective-permute-start
  60.5 4.9 %collective-permute-done = bf16[16,2048]{1,0:T(8,128)(2,1)S(1)} collective-permute-done((bf16[16,2048]{1,0:T(8,128)(2,1)S(1)}, bf16[16,2048]{1,0:T(8,128)(2,1)S(1)}, u32[]{:S(2)}, u32[]{:S(2)}) %collective-permute-start) | collective-permute-done | bytes 65568 | tf_op jit(solution)/shard_map/ppermute | solution.py:257
  65.3 1.5 collective-permute-start.1
  66.8 2.5 %collective-permute-done.1 = bf16[32,2048]{1,0:T(8,128)(2,1)S(1)} collective-permute-done((bf16[32,2048]{1,0:T(8,128)(2,1)S(1)}, bf16[32,2048]{1,0:T(8,128)(2,1)S(1)}, u32[]{:S(2)}, u32[]{:S(2)}) %collective-permute-start.1) | collective-permute-done | bytes 131104 | tf_op jit(solution)/shard_map/ppermute | solution.py:258
  70.1 2.0 all-gather
  72.2 48.0 %all-gather.3.cloned.1.call-done = bf16[64,64,2048]{2,1,0:T(8,128)(2,1)} async-done(((bf16[1,64,2048]{2,1,0:T(8,128)(2,1)}), bf16[64,64,2048]{2,1,0:T(8,128)(2,1)}) %all-gather.3.cloned.1.call-update) | async-done | bytes 16777232 | tf_op jit(solution)/shard_map/all_gather | solution.py:305
  120.2 6.0 %first_stage.1 = (bf16[32,2048]{1,0:T(8,128)(2,1)S(1)}, bf16[32,2,64,2048]{3,2,1,0:T(8,128)(2,1)S(1)}) custom-call(s32[1]{0:T(128)} %bitcast.position_ref, bf16[128,2048]{1,0:T(8,128)(2,1)S(1)} %pad_maximum_fusion.queue_ref.refs_0_, f32[2,2048]{1,0:T(2,128)S(1)} %bitcast.8, bf16[32,2,64,2048]{3,2,1,0:T(8,128)(2,1)} %bitcast.28), custom_call_target="tpu_custom_call" | custom-call | tf_op jit(solution)/shard_map/first_stage/pallas_call | solution.py:174
  133.2 1.3 collective-permute-start.8
  134.5 1.3 collective-permute-start.16
  135.8 44.7 %collective-permute-done.8.refs_0_ = bf16[32,2048]{1,0:T(8,128)(2,1)S(1)} collective-permute-done((bf16[32,2048]{1,0:T(8,128)(2,1)S(1)}, bf16[32,2048]{1,0:T(8,128)(2,1)S(1)}, u32[]{:S(2)}, u32[]{:S(2)}) %collective-permute-start.8) | collective-permute-done | bytes 131104 | tf_op jit(solution)/shard_map/ppermute | solution.py:281
  180.6 3.7 %stage.22.refs_0_ = bf16[32,2048]{1,0:T(8,128)(2,1)S(1)} custom-call(s32[1]{0:T(128)} %bitcast.position_ref, bf16[32,2048]{1,0:T(8,128)(2,1)S(1)} %collective-permute-done.8.refs_0_, f32[2,2048]{1,0:T(2,128)S(1)} %bitcast.20, bf16[32,2,64,2048]{3,2,1,0:T(8,128)(2,1)S(1)} %get-tuple-element.8.refs_3_.refs_2_), custom_call_target="tpu_custom_call" | custom-call | tf_op jit(solution)/shard_map/stage/pallas_call | solution.py:220
  184.3 1.9 collective-permute-start.9
  186.7 3.7 %stage.30 = bf16[32,2048]{1,0:T(8,128)(2,1)S(1)} custom-call(s32[1]{0:T(128)} %bitcast.position_ref, bf16[32,2048]{1,0:T(8,128)(2,1)S(1)} %stage.22.refs_0_, bf16[32,2048]{1,0:T(8,128)(2,1)S(1)} %collective-permute-done.16.refs_1_, f32[2,2048]{1,0:T(2,128)S(1)} %bitcast.21, bf16[32,2,64,2048]{3,2,1,0:T(8,128)(2,1)S(1)} %get-tuple-element.8.refs_3_.refs_2_), custom_call_target="tpu_custom_call" | custom-call | tf_op jit(solution)/shard_map/stage/pallas_call | solution.py:220
  190.4 1.9 collective-permute-start.17
  192.4 3.7 %stage.23.refs_0_ = bf16[32,2048]{1,0:T(8,128)(2,1)S(1)} custom-call(s32[1]{0:T(128)} %bitcast.position_ref, bf16[32,2048]{1,0:T(8,128)(2,1)S(1)} %collective-permute-done.9.refs_0_, f32[2,2048]{1,0:T(2,128)S(1)} %bitcast.22, bf16[32,2,64,2048]{3,2,1,0:T(8,128)(2,1)S(1)} %get-tuple-element.8.refs_3_.refs_2_), custom_call_target="tpu_custom_call" | custom-call | tf_op jit(solution)/shard_map/stage/pallas_call | solution.py:220
  196.1 1.8 collective-permute-start.10
  197.9 3.7 %stage.31 = bf16[32,2048]{1,0:T(8,128)(2,1)S(1)} custom-call(s32[1]{0:T(128)} %bitcast.position_ref, bf16[32,2048]{1,0:T(8,128)(2,1)S(1)} %stage.23.refs_0_, bf16[32,2048]{1,0:T(8,128)(2,1)S(1)} %collective-permute-done.17.refs_1_, f32[2,2048]{1,0:T(2,128)S(1)} %bitcast.23, bf16[32,2,64,2048]{3,2,1,0:T(8,128)(2,1)S(1)} %get-tuple-element.8.refs_3_.refs_2_), custom_call_target="tpu_custom_call" | custom-call | tf_op jit(solution)/shard_map/stage/pallas_call | solution.py:220
  201.6 2.0 collective-permute-start.18
  205.0 1.1 collective-permute-done.18.refs_1_
  206.1 1.3 collective-permute-start.21
  208.1 9.8 %collective-permute-done.21.refs_4_ = bf16[32,2048]{1,0:T(8,128)(2,1)S(1)} collective-permute-done((bf16[32,2048]{1,0:T(8,128)(2,1)S(1)}, bf16[32,2048]{1,0:T(8,128)(2,1)S(1)}, u32[]{:S(2)}, u32[]{:S(2)}) %collective-permute-start.21) | collective-permute-done | bytes 131104 | tf_op jit(solution)/shard_map/ppermute | solution.py:281
  (63 shorter events, 14.6 us)
Async XLA Ops:
  6.5 113.6 %all-gather.3.cloned.1.call-start = ((), (), s32[]{:S(2)}) async-start(), calls=%async_computation.2 | async-start | bytes 17039360 | tf_op jit(solution)/shard_map/all_gather | solution.py:305
  59.2 6.2 %collective-permute-start = (bf16[16,2048]{1,0:T(8,128)(2,1)S(1)}, bf16[16,2048]{1,0:T(8,128)(2,1)S(1)}, u32[]{:S(2)}, u32[]{:S(2)}) collective-permute-start(bf16[16,2048]{1,0:T(8,128)(2,1)S(1)} %reduce_sum.12), channel_id=1, source_target_pairs={{2,0},{6,4},{10,8},{14,12},{3,1},{7,5},{11,9},{15,13},{18,16},{22,... | collective-permute-start | bytes 196616 | tf_op jit(solution)/shard_map/ppermute | solution.py:257
  65.3 4.0 %collective-permute-start.1 = (bf16[32,2048]{1,0:T(8,128)(2,1)S(1)}, bf16[32,2048]{1,0:T(8,128)(2,1)S(1)}, u32[]{:S(2)}, u32[]{:S(2)}) collective-permute-start(bf16[32,2048]{1,0:T(8,128)(2,1)S(1)} %pad_maximum_fusion.2), channel_id=1, source_target_pairs={{4,0},{12,8},{5,1},{13,9},{20,16},{28,24},{21,17},{29,25},{36,32},... | collective-permute-start | bytes 393224 | tf_op jit(solution)/shard_map/ppermute | solution.py:258
  69.4 2.7 %collective-permute-start.2 = (bf16[64,2048]{1,0:T(8,128)(2,1)S(1)}, bf16[64,2048]{1,0:T(8,128)(2,1)S(1)}, u32[]{:S(2)}, u32[]{:S(2)}) collective-permute-start(bf16[64,2048]{1,0:T(8,128)(2,1)S(1)} %pad_maximum_fusion.1), channel_id=1, source_target_pairs={{8,0},{9,1},{24,16},{25,17},{40,32},{41,33},{56,48},{57,49},{72,64... | collective-permute-start | bytes 786440 | tf_op jit(solution)/shard_map/ppermute | solution.py:259
  126.2 1.4 collective-permute-start.3
  126.9 1.4 collective-permute-start.11
  127.6 1.4 collective-permute-start.4
  128.3 1.4 collective-permute-start.12
  129.0 1.4 collective-permute-start.5
  129.7 1.4 collective-permute-start.13
  130.4 1.4 collective-permute-start.6
  131.1 1.4 collective-permute-start.14
  131.8 1.4 collective-permute-start.7
  132.5 2.0 collective-permute-start.15
  133.2 47.3 %collective-permute-start.8 = (bf16[32,2048]{1,0:T(8,128)(2,1)S(1)}, bf16[32,2048]{1,0:T(8,128)(2,1)S(1)}, u32[]{:S(2)}, u32[]{:S(2)}) collective-permute-start(bf16[32,2048]{1,0:T(8,128)(2,1)S(1)} %stage.21.refs_0_), channel_id=1, source_target_pairs={{8,10},{10,12},{9,11},{11,13},{24,26},{26,28},{25,27},{27,29},{40,... | collective-permute-start | bytes 393224 | tf_op jit(solution)/shard_map/ppermute | solution.py:281
  134.5 52.2 %collective-permute-start.16 = (bf16[32,2048]{1,0:T(8,128)(2,1)S(1)}, bf16[32,2048]{1,0:T(8,128)(2,1)S(1)}, u32[]{:S(2)}, u32[]{:S(2)}) collective-permute-start(bf16[32,2048]{1,0:T(8,128)(2,1)S(1)} %stage.29), channel_id=1, source_target_pairs={{8,10},{10,12},{9,11},{11,13},{24,26},{26,28},{25,27},{27,29},{40,... | collective-permute-start | bytes 393224 | tf_op jit(solution)/shard_map/ppermute | solution.py:281
  184.3 8.1 %collective-permute-start.9 = (bf16[32,2048]{1,0:T(8,128)(2,1)S(1)}, bf16[32,2048]{1,0:T(8,128)(2,1)S(1)}, u32[]{:S(2)}, u32[]{:S(2)}) collective-permute-start(bf16[32,2048]{1,0:T(8,128)(2,1)S(1)} %stage.22.refs_0_), channel_id=1, source_target_pairs={{10,12},{12,14},{11,13},{13,15},{26,28},{28,30},{27,29},{29,31},{4... | collective-permute-start | bytes 393224 | tf_op jit(solution)/shard_map/ppermute | solution.py:281
  190.4 7.5 %collective-permute-start.17 = (bf16[32,2048]{1,0:T(8,128)(2,1)S(1)}, bf16[32,2048]{1,0:T(8,128)(2,1)S(1)}, u32[]{:S(2)}, u32[]{:S(2)}) collective-permute-start(bf16[32,2048]{1,0:T(8,128)(2,1)S(1)} %stage.30), channel_id=1, source_target_pairs={{10,12},{12,14},{11,13},{13,15},{26,28},{28,30},{27,29},{29,31},{4... | collective-permute-start | bytes 393224 | tf_op jit(solution)/shard_map/ppermute | solution.py:281
  196.1 7.5 %collective-permute-start.10 = (bf16[32,2048]{1,0:T(8,128)(2,1)S(1)}, bf16[32,2048]{1,0:T(8,128)(2,1)S(1)}, u32[]{:S(2)}, u32[]{:S(2)}) collective-permute-start(bf16[32,2048]{1,0:T(8,128)(2,1)S(1)} %stage.23.refs_0_), channel_id=1, source_target_pairs={{12,14},{14,0},{13,15},{15,1},{28,30},{30,16},{29,31},{31,17},{44,... | collective-permute-start | bytes 393224 | tf_op jit(solution)/shard_map/ppermute | solution.py:281
  201.6 4.5 %collective-permute-start.18 = (bf16[32,2048]{1,0:T(8,128)(2,1)S(1)}, bf16[32,2048]{1,0:T(8,128)(2,1)S(1)}, u32[]{:S(2)}, u32[]{:S(2)}) collective-permute-start(bf16[32,2048]{1,0:T(8,128)(2,1)S(1)} %stage.31), channel_id=1, source_target_pairs={{12,14},{14,4},{13,15},{15,5},{28,30},{30,20},{29,31},{31,21},{44,... | collective-permute-start | bytes 393224 | tf_op jit(solution)/shard_map/ppermute | solution.py:281
  203.6 3.8 %collective-permute-start.20 = (bf16[32,2048]{1,0:T(8,128)(2,1)S(1)}, bf16[32,2048]{1,0:T(8,128)(2,1)S(1)}, u32[]{:S(2)}, u32[]{:S(2)}) collective-permute-start(bf16[32,2048]{1,0:T(8,128)(2,1)S(1)} %stage.32.refs_0_), channel_id=1, source_target_pairs={{14,10},{15,11},{30,26},{31,27},{46,42},{47,43},{62,58},{63,59},{7... | collective-permute-start | bytes 393224 | tf_op jit(solution)/shard_map/ppermute | solution.py:281
  204.3 3.1 %collective-permute-start.19 = (bf16[32,2048]{1,0:T(8,128)(2,1)S(1)}, bf16[32,2048]{1,0:T(8,128)(2,1)S(1)}, u32[]{:S(2)}, u32[]{:S(2)}) collective-permute-start(bf16[32,2048]{1,0:T(8,128)(2,1)S(1)} %stage.32.refs_0_), channel_id=1, source_target_pairs={{14,8},{15,9},{30,24},{31,25},{46,40},{47,41},{62,56},{63,57},{78,... | collective-permute-start | bytes 393224 | tf_op jit(solution)/shard_map/ppermute | solution.py:285
  206.1 11.8 %collective-permute-start.21 = (bf16[32,2048]{1,0:T(8,128)(2,1)S(1)}, bf16[32,2048]{1,0:T(8,128)(2,1)S(1)}, u32[]{:S(2)}, u32[]{:S(2)}) collective-permute-start(bf16[32,2048]{1,0:T(8,128)(2,1)S(1)} %stage.33.refs_6_), channel_id=1, source_target_pairs={{14,12},{15,13},{30,28},{31,29},{46,44},{47,45},{62,60},{63,61},{7... | collective-permute-start | bytes 393224 | tf_op jit(solution)/shard_map/ppermute | solution.py:281
  207.4 10.5 %collective-permute-start.22 = (bf16[16,2048]{1,0:T(8,128)(2,1)S(1)}, bf16[16,2048]{1,0:T(8,128)(2,1)S(1)}, u32[]{:S(2)}, u32[]{:S(2)}) collective-permute-start(bf16[16,2048]{1,0:T(8,128)(2,1)S(1)} %choose.2), channel_id=1, source_target_pairs={{0,2},{4,6},{1,3},{5,7},{16,18},{20,22},{17,19},{21,23},{32,34},{3... | collective-permute-start | bytes 196616 | tf_op jit(solution)/shard_map/ppermute | solution.py:288
  (4 other events, 3.2 us)
Sparse Core Ops, SparseCore 0:
  10.7 109.4 all-gather.2
